TPU v7x, 32 devices: a whole 2x2x4 slice. The times are simulated.
32 devices in a mesh: clip: 4 (over y, core), frame: 8 (over z, x).
Axes of the slice: x: 2, y: 2, z: 4, core: 2. Of those that a mesh axis runs over, the one named last changes fastest.
Arguments:
- video: bfloat16 [128, 512, 512], P(('clip', 'frame')), parts along dimension 0, may hold values from -6 to 6
- timestep: int32 [4], P('clip'), parts along dimension 0, may hold values from 0 to 999
- cond_weight: bfloat16 [128, 2048], replicated, may hold values from -0.5 to 0.5
- spatial_gain: float32 [512], replicated, may hold values from 0.25 to 1.75
- spatial_qkv: bfloat16 [512, 1536], replicated, may hold values from -0.25 to 0.25
- spatial_out: bfloat16 [512, 512], replicated, may hold values from -0.25 to 0.25
- temporal_gain: float32 [512], replicated, may hold values from 0.25 to 1.75
- temporal_qkv: bfloat16 [512, 1536], replicated, may hold values from -0.25 to 0.25
- temporal_out: bfloat16 [512, 512], replicated, may hold values from -0.25 to 0.25
- merge_weight: bfloat16 [4096, 1024], replicated, may hold values from -0.09375 to 0.09375
- coarse_gain: float32 [1024], replicated, may hold values from 0.25 to 1.75
- coarse_qkv: bfloat16 [1024, 3072], replicated, may hold values from -0.1875 to 0.1875
- coarse_out: bfloat16 [1024, 1024], replicated, may hold values from -0.1875 to 0.1875
- up_weight: bfloat16 [1024, 512], replicated, may hold values from -0.1875 to 0.1875
Outputs:
- denoised: bfloat16 [128, 512, 512], P(('clip', 'frame')), parts along dimension 0
There are 4 independent parts, one for each index of `clip`. A program takes and returns all parts, laid end to end along the dimension named above; an argument that names none is the same for every part. Nothing has to cross between parts.
All inputs are finite; a program needn't handle non-finite values.
Results may differ from a plain program's by a relative error of at most 0.015.
Values may be sent and summed in bfloat16 or wider, within the bound.
No kernel may reach another device: no remote copies, remote signals or barrier semaphores. Data moves between devices by JAX's collectives and lax.ppermute only.
A program may use at most 192 MiB of HBM per device.

v0:
```python
import math

import jax
import jax.numpy as jnp
from jax import lax
from jax.sharding import PartitionSpec as P

D = 512
DC = 1024
HEAD = 64
FREQ = 64


def modulation_of(timestep, cond_weight):
    counter = jnp.arange(FREQ, dtype=jnp.float32)
    frequency = jnp.exp(counter * (-math.log(10000.0) / FREQ))
    angles = timestep.astype(jnp.float32)[0] * frequency
    embedding = jnp.concatenate([jnp.sin(angles), jnp.cos(angles)])
    return jnp.dot(
        embedding[None, :], cond_weight.astype(jnp.float32), precision=lax.Precision.HIGHEST
    )[0]


def attention_block(inputs, gain_vec, scale_mod, shift_mod, w_qkv, w_out, head_count):
    length, batched, features = inputs.shape
    widened = inputs.astype(jnp.float32)
    mean_square = jnp.mean(widened * widened, axis=-1, keepdims=True)
    normed = (
        widened * lax.rsqrt(mean_square + 1e-06) * gain_vec * (1.0 + scale_mod) + shift_mod
    ).astype(jnp.bfloat16)
    projected = jnp.dot(
        normed.reshape(length * batched, features), w_qkv, preferred_element_type=jnp.float32
    )
    projected = projected.astype(jnp.bfloat16).reshape(
        length, batched, 3, head_count, features // head_count
    )
    queries = projected[:, :, 0]
    keys = projected[:, :, 1]
    values = projected[:, :, 2]
    scores = jnp.einsum("snhe,tnhe->nhst", queries, keys, preferred_element_type=jnp.float32) * (
        1.0 / math.sqrt(features // head_count)
    )
    probs = jax.nn.softmax(scores, axis=-1).astype(jnp.bfloat16)
    mixed = jnp.einsum("nhst,tnhe->snhe", probs, values, preferred_element_type=jnp.float32)
    mixed = mixed.astype(jnp.bfloat16).reshape(length * batched, features)
    update = jnp.dot(mixed, w_out, preferred_element_type=jnp.float32).reshape(
        length, batched, features
    )
    return (widened + update).astype(jnp.bfloat16)


def merge_frames(fine_tokens, merge_weight):
    frames_here, blocks, quads, features = fine_tokens.shape
    paired = fine_tokens.reshape(frames_here // 2, 2, blocks, quads, features).transpose(
        0, 2, 1, 3, 4
    )
    paired = paired.reshape(frames_here // 2 * blocks, 2 * quads * features)
    merged = jnp.dot(paired, merge_weight, preferred_element_type=jnp.float32).astype(jnp.bfloat16)
    return merged.reshape(frames_here // 2, blocks, merge_weight.shape[1])


def combine_levels(fine_tokens, coarse_tokens, up_weight):
    frames_here, blocks, quads, features = fine_tokens.shape
    upsampled = jnp.dot(
        coarse_tokens.reshape(-1, coarse_tokens.shape[2]),
        up_weight,
        preferred_element_type=jnp.float32,
    )
    upsampled = upsampled.reshape(frames_here // 2, 1, blocks, 1, features)
    result = (
        fine_tokens.astype(jnp.float32).reshape(frames_here // 2, 2, blocks, quads, features)
        + upsampled
    )
    return result.astype(jnp.bfloat16).reshape(fine_tokens.shape)


def body(
    video,
    timestep,
    cond_weight,
    spatial_gain,
    spatial_qkv,
    spatial_out,
    temporal_gain,
    temporal_qkv,
    temporal_out,
    merge_weight,
    coarse_gain,
    coarse_qkv,
    coarse_out,
    up_weight,
):
    frames_local, tokens_frame, features = video.shape
    groups = lax.axis_size("frame")
    cells_local = tokens_frame // 4 // groups
    modulation = modulation_of(timestep, cond_weight)
    scale_s, shift_s, scale_t, shift_t = [modulation[i * D : (i + 1) * D] for i in range(4)]

    def spatial(frame_rows):
        return attention_block(
            frame_rows[:, None, :],
            spatial_gain,
            scale_s,
            shift_s,
            spatial_qkv,
            spatial_out,
            D // HEAD,
        )[:, 0, :]

    fine1 = lax.map(spatial, video)
    grouped = fine1.reshape(frames_local, groups, cells_local, 4, features)
    cell_view = lax.all_to_all(grouped, "frame", split_axis=1, concat_axis=0, tiled=True)
    length = cell_view.shape[0]
    single = cell_view.shape[1]
    blocks = cell_view.shape[2]
    cell_rows = cell_view.reshape(length, single * blocks, 4, features)
    temporal_length = cell_rows.shape[0]
    temporal_blocks = cell_rows.shape[1]
    mixed = attention_block(
        cell_rows.reshape(temporal_length, temporal_blocks * 4, features),
        temporal_gain,
        scale_t,
        shift_t,
        temporal_qkv,
        temporal_out,
        D // HEAD,
    )
    fine2 = mixed.reshape(cell_rows.shape)
    coarse0 = merge_frames(fine2, merge_weight)
    coarse1 = attention_block(coarse0, coarse_gain, 0.0, 0.0, coarse_qkv, coarse_out, DC // HEAD)
    exchanged = combine_levels(fine2, coarse1, up_weight).reshape(cell_view.shape)
    result = lax.all_to_all(exchanged, "frame", split_axis=0, concat_axis=1, tiled=True)
    return result.reshape(frames_local, tokens_frame, features)


def solution(mesh):
    return jax.shard_map(
        body,
        mesh=mesh,
        in_specs=(
            P(("clip", "frame"), None, None),
            P("clip"),
            P(),
            P(),
            P(),
            P(),
            P(),
            P(),
            P(),
            P(),
            P(),
            P(),
            P(),
            P(),
        ),
        out_specs=P(("clip", "frame"), None, None),
        check_vma=False,
    )
```

profile of v0, /device:TPU:0, one launch (start us, length us, event | category | flops | bytes accessed | tf_op | source)
XLA Modules:
  0.0 348.0 jit_solution(16680445970739835808)
XLA Ops:
  2.3 87.0 %while.10 = (s32[]{:T(128)}, bf16[4,512,512]{2,1,0:T(8,128)(2,1)}, bf16[4,512,512]{2,1,0:T(8,128)(2,1)}, f32[512]{0:T(512)}, f32[512]{0:T(512)S(1)}, /*index=5*/...) while((s32[]{:T(128)}, bf16[4,512,512]{2,1,0:T(8,128)(2,1)}, ...), condition=%wide.region_4.5_spmd, body=%wide.region_0.4_spmd.sunk | while | flops 1625294336 | bytes 30460044 | solution.py:110
  10.0 7.2 %fusion.99 = (f32[8,512]{1,0:T(8,128)S(1)}, f32[8,512,512]{1,2,0:T(8,128)}) fusion(bf16[512,1,3,8,64]{0,4,3,2,1:T(8,128)(2,1)} %bitcast.178), kind=kOutput, calls=%fused_computation.101.clone.1 | convolution fusion | flops 274727424 | bytes 9453568 | tf_op jit(solution)/shard_map/while/body/eval_jaxpr/sub | solution.py:43
  17.2 4.5 %fusion.100 = bf16[8,64,512]{2,1,0:T(8,128)(2,1)S(1)} fusion(f32[8,512,512]{1,2,0:T(8,128)} %get-tuple-element.141, f32[8,512]{1,0:T(8,128)S(1)} %get-tuple-element.142, bf16[512,1,3,8,64]{0,4,3,2,1:T(8,128)(2,1)} %bitcast.179), kind=kOutput, calls=%fused_computation.12.clone.1 | convolution fusion | flops 272891904 | bytes 9453568 | tf_op jit(solution)/shard_map/while/body/eval_jaxpr/nhst,tnhe->snhe/dot_general | solution.py:44
  31.7 7.2 %fusion.99 = (f32[8,512]{1,0:T(8,128)S(1)}, f32[8,512,512]{1,2,0:T(8,128)}) fusion(bf16[512,1,3,8,64]{0,4,3,2,1:T(8,128)(2,1)} %bitcast.178), kind=kOutput, calls=%fused_computation.101.clone.1 | convolution fusion | flops 274727424 | bytes 9453568 | tf_op jit(solution)/shard_map/while/body/eval_jaxpr/sub | solution.py:43
  53.5 7.2 %fusion.99 = (f32[8,512]{1,0:T(8,128)S(1)}, f32[8,512,512]{1,2,0:T(8,128)}) fusion(bf16[512,1,3,8,64]{0,4,3,2,1:T(8,128)(2,1)} %bitcast.178), kind=kOutput, calls=%fused_computation.101.clone.1 | convolution fusion | flops 274727424 | bytes 9453568 | tf_op jit(solution)/shard_map/while/body/eval_jaxpr/sub | solution.py:43
  75.2 7.2 %fusion.99 = (f32[8,512]{1,0:T(8,128)S(1)}, f32[8,512,512]{1,2,0:T(8,128)}) fusion(bf16[512,1,3,8,64]{0,4,3,2,1:T(8,128)(2,1)} %bitcast.178), kind=kOutput, calls=%fused_computation.101.clone.1 | convolution fusion | flops 274727424 | bytes 9453568 | tf_op jit(solution)/shard_map/while/body/eval_jaxpr/sub | solution.py:43
  95.7 55.8 %all_to_all.24 = bf16[4,8,16,4,512]{4,3,2,0,1:T(4,128)(2,1)S(1)} all-to-all(bf16[4,8,16,4,512]{4,3,2,0,1:T(4,128)(2,1)S(1)} %copy.46), channel_id=1, replica_groups=mesh['clip'=4,'frame'=8] {'frame'}, dimensions={1} | all-to-all | bytes 4194304 | tf_op jit(solution)/shard_map/all_to_all | solution.py:112
  155.5 5.3 %reshape.246 = f32[2048,512]{1,0:T(8,128)} reshape(f32[8,4,1,16,4,512]{5,4,3,1,0,2:T(4,128)} %convert_bitcast_fusion.1) | data formatting | bytes 8388608 | tf_op jit(solution)/shard_map/convert_element_type | solution.py:26
  160.7 5.3 %reshape.245 = f32[32,64,512]{2,1,0:T(8,128)} reshape(f32[8,4,1,16,4,512]{5,4,3,1,0,2:T(4,128)} %convert_bitcast_fusion.1) | data formatting | bytes 8388608 | tf_op jit(solution)/shard_map/convert_element_type | solution.py:26
  169.0 8.9 %convolution_convert_fusion.1 = bf16[2048,1536]{1,0:T(8,128)(2,1)} fusion(bf16[512,1536]{1,0:T(8,128)(2,1)} %param.23, f32[2048,512]{1,0:T(8,128)} %reshape.246, f32[512]{0:T(512)S(1)} %get-tuple-element.75, f32[512]{0:T(512)S(1)} %get-tuple-element.74, f32[512]{0:T(512)S(1)} %copy-done.5, f32[2048]{0:T(1024)S(1)} %rsqrt.28), kind=kOutput, calls=%fused_computation.39 | convolution fusion | flops 3229614080 | bytes 12072960 | tf_op jit(solution)/shard_map/dot_general | solution.py:31
  177.9 16.2 %reshape.240 = bf16[32,64,3,8,64]{4,3,2,1,0:T(8,128)(2,1)} reshape(bf16[2048,1536]{1,0:T(8,128)(2,1)} %convolution_convert_fusion.1) | data formatting | bytes 12582912 | tf_op jit(solution)/shard_map/reshape | solution.py:34
  194.2 7.3 %fusion.72 = (bf16[32,64,1,8,64]{4,3,2,1,0:T(8,128)(2,1)}, bf16[32,64,1,8,64]{4,3,2,1,0:T(8,128)(2,1)S(1)}, bf16[32,64,1,8,64]{4,3,2,1,0:T(8,128)(2,1)S(1)}) fusion(bf16[32,64,3,8,64]{4,3,2,1,0:T(8,128)(2,1)} %reshape.240), kind=kLoop, calls=%fused_computation.102 | loop fusion | bytes 12582912 | tf_op jit(solution)/shard_map/slice | solution.py:39
  201.5 5.4 %fusion.34 = f32[64,8,32,32]{2,3,1,0:T(8,128)S(1)} fusion(bf16[32,64,1,8,64]{4,3,2,1,0:T(8,128)(2,1)S(1)} %get-tuple-element.70, bf16[32,64,1,8,64]{4,3,2,1,0:T(8,128)(2,1)S(1)} %get-tuple-element.69), kind=kOutput, calls=%fused_computation.47 | convolution fusion | flops 67108864 | bytes 6291456 | tf_op jit(solution)/shard_map/snhe,tnhe->nhst/dot_general | solution.py:40
  206.9 5.0 %fusion.74 = (f32[64,8,32]{2,1,0:T(8,128)S(1)}, f32[64,8,32,32]{2,3,1,0:T(8,128)}) fusion(f32[64,8,32,32]{2,3,1,0:T(8,128)S(1)} %fusion.34), kind=kOutput, calls=%fused_computation.104 | output fusion | flops 2097183 | bytes 4259840 | tf_op jit(solution)/shard_map/sub | solution.py:43
  211.8 8.2 %convert_bitcast_fusion.2 = bf16[32,64,8,64]{3,0,2,1:T(8,128)(2,1)S(1)} fusion(f32[64,8,32,32]{2,3,1,0:T(8,128)} %get-tuple-element.79, f32[64,8,32]{2,1,0:T(8,128)S(1)} %get-tuple-element.78, bf16[32,64,1,8,64]{4,3,2,1,0:T(8,128)(2,1)} %get-tuple-element.68), kind=kOutput, calls=%fused_computation.53 | convolution fusion | flops 69206016 | bytes 6356992 | tf_op jit(solution)/shard_map/nhst,tnhe->snhe/dot_general | solution.py:44
  223.6 6.5 %dot_general.53 = bf16[32,64,512]{2,1,0:T(8,128)(2,1)} reshape(bf16[32,64,8,64]{3,2,1,0:T(8,128)(2,1)} %copy.51) | data formatting | bytes 4194304 | tf_op jit(solution)/shard_map/dot_general | solution.py:46
  230.1 5.4 %add_convert_fusion = bf16[32,64,512]{2,1,0:T(8,128)(2,1)} fusion(f32[32,64,512]{2,1,0:T(8,128)} %reshape.245, bf16[32,64,512]{2,1,0:T(8,128)(2,1)} %dot_general.53, bf16[512,512]{1,0:T(8,128)(2,1)S(1)} %copy-done.2), kind=kOutput, calls=%fused_computation.52 | convolution fusion | flops 1075838976 | bytes 8912896 | tf_op jit(solution)/shard_map/dot_general | solution.py:46
  239.4 4.8 %reshape.247 = f32[32,1,16,4,512]{4,3,2,0,1:T(4,128)} reshape(bf16[32,64,512]{2,1,0:T(8,128)(2,1)} %add_convert_fusion) | data formatting | bytes 6291456 | tf_op jit(solution)/shard_map/convert_element_type | solution.py:71
  248.0 4.7 %reshape.241 = bf16[256,4096]{1,0:T(8,128)(2,1)} reshape(bf16[16,16,2,4,512]{4,3,2,1,0:T(4,128)(2,1)} %bitcast.180) | data formatting | bytes 4194304 | tf_op jit(solution)/shard_map/reshape | solution.py:57
  252.7 6.4 %multiply_reduce_fusion.3 = (f32[256]{0:T(256)S(1)}, f32[256,1024]{1,0:T(8,128)S(1)}) fusion(bf16[256,4096]{1,0:T(8,128)(2,1)} %reshape.241, bf16[4096,1024]{1,0:T(8,128)(2,1)} %param.25), kind=kOutput, calls=%fused_computation.84 | convolution fusion | flops 2148531968 | bytes 11535360 | tf_op jit(solution)/shard_map/dot_general | solution.py:58
  260.1 5.8 %convolution_convert_fusion.2 = bf16[256,3072]{1,0:T(8,128)(2,1)} fusion(bf16[1024,3072]{1,0:T(8,128)(2,1)} %param.27, f32[256,1024]{1,0:T(8,128)S(1)} %get-tuple-element.81, f32[1024]{0:T(1024)S(1)} %copy-done.4, f32[256]{0:T(256)S(1)} %add_rsqrt_fusion.1), kind=kOutput, calls=%fused_computation.57 | convolution fusion | flops 1612185600 | bytes 8918016 | tf_op jit(solution)/shard_map/dot_general | solution.py:31
  265.9 4.9 %reshape.242 = bf16[16,16,3,16,64]{4,3,2,1,0:T(8,128)(2,1)} reshape(bf16[256,3072]{1,0:T(8,128)(2,1)} %convolution_convert_fusion.2) | data formatting | bytes 3145728 | tf_op jit(solution)/shard_map/reshape | solution.py:34
  274.9 4.8 %fusion.75 = (f32[16,16,16]{2,1,0:T(8,128)S(1)}, f32[16,16,16,16]{2,3,1,0:T(8,128)}) fusion(bf16[16,16,1,16,64]{4,3,2,1,0:T(8,128)(2,1)} %get-tuple-element.73, bf16[16,16,1,16,64]{4,3,2,1,0:T(8,128)(2,1)} %get-tuple-element.72), kind=kOutput, calls=%fused_computation.105 | convolution fusion | flops 8585231 | bytes 1327104 | tf_op jit(solution)/shard_map/sub | solution.py:43
  290.2 51.4 %all_to_all.25 = bf16[32,1,16,4,512]{4,3,2,1,0:T(4,128)(2,1)S(1)} all-to-all(bf16[32,1,16,4,512]{4,3,2,1,0:T(4,128)(2,1)S(1)} %fusion.35), channel_id=1, replica_groups=mesh['clip'=4,'frame'=8] {'frame'}, dimensions={0} | all-to-all | bytes 4194304 | tf_op jit(solution)/shard_map/all_to_all | solution.py:132
  (66 shorter events, 101.3 us)
Async XLA Ops:
  0.0 283.9 %copy-start = (bf16[1024,1024]{1,0:T(8,128)(2,1)S(1)}, bf16[1024,1024]{1,0:T(8,128)(2,1)}, u32[]{:S(2)}) copy-start(bf16[1024,1024]{1,0:T(8,128)(2,1)} %param.28) | copy-start | bytes 6291460
  17.2 4.5 %copy-start.3 = (bf16[512,512]{1,0:T(8,128)(2,1)S(1)}, bf16[512,512]{1,0:T(8,128)(2,1)}, u32[]{:S(2)}) copy-start(bf16[512,512]{1,0:T(8,128)(2,1)} %get-tuple-element.168) | copy-start | bytes 1572868 | tf_op jit(solution)/shard_map/while
  39.0 4.5 %copy-start.3 = (bf16[512,512]{1,0:T(8,128)(2,1)S(1)}, bf16[512,512]{1,0:T(8,128)(2,1)}, u32[]{:S(2)}) copy-start(bf16[512,512]{1,0:T(8,128)(2,1)} %get-tuple-element.168) | copy-start | bytes 1572868 | tf_op jit(solution)/shard_map/while
  60.7 4.5 %copy-start.3 = (bf16[512,512]{1,0:T(8,128)(2,1)S(1)}, bf16[512,512]{1,0:T(8,128)(2,1)}, u32[]{:S(2)}) copy-start(bf16[512,512]{1,0:T(8,128)(2,1)} %get-tuple-element.168) | copy-start | bytes 1572868 | tf_op jit(solution)/shard_map/while
  82.5 4.5 %copy-start.3 = (bf16[512,512]{1,0:T(8,128)(2,1)S(1)}, bf16[512,512]{1,0:T(8,128)(2,1)}, u32[]{:S(2)}) copy-start(bf16[512,512]{1,0:T(8,128)(2,1)} %get-tuple-element.168) | copy-start | bytes 1572868 | tf_op jit(solution)/shard_map/while
  151.5 1.3 copy-start.1
  160.7 8.3 %copy-start.5 = (f32[512]{0:T(512)S(1)}, f32[512]{0:T(512)}, u32[]{:S(2)}) copy-start(f32[512]{0:T(512)} %param.22) | copy-start | bytes 6148
  223.6 6.5 %copy-start.2 = (bf16[512,512]{1,0:T(8,128)(2,1)S(1)}, bf16[512,512]{1,0:T(8,128)(2,1)}, u32[]{:S(2)}) copy-start(bf16[512,512]{1,0:T(8,128)(2,1)} %param.24) | copy-start | bytes 1572868
  252.7 7.4 %copy-start.4 = (f32[1024]{0:T(1024)S(1)}, f32[1024]{0:T(1024)}, u32[]{:S(2)}) copy-start(f32[1024]{0:T(1024)} %param.26) | copy-start | bytes 12292
  259.1 1.0 copy-start.6
where the time goes:
time: 355 us; the launch traced here: 348 us
  matrix products  123 us (35%)
  blocking collectives  107 us (30%)
  local copies, waits for them, and re-layouts  98 us (28%)
  other arithmetic  18.8 us (5%)
    all_to_all x1, blocking collectives, body(): lax.all_to_all(grouped, 'frame', split_axis=1, concat_axis=0, tiled=True)  55.8 us
    all_to_all x1, blocking collectives, body(): lax.all_to_all(exchanged, 'frame', split_axis=0, concat_axis=1, tiled=True)  51.4 us
    sub x5, matrix products, attention_block(): probs = jax.nn.softmax(scores, axis=-1).astype(jnp.bfloat16)  33.7 us
    dot_general x6, matrix products, attention_block(): jnp.dot(normed.reshape(length * batched, features), w_qkv, preferred_elem...  30 us
    dot_general x6, matrix products, attention_block(): jnp.einsum('nhst,tnhe->snhe', probs, values, preferred_element_type=jnp.f...  28.5 us
    reshape x2, local copies, waits for them, and re-layouts, attention_block(): projected.astype(jnp.bfloat16)  21.1 us
    dot_general x5, matrix products, attention_block(): jnp.dot(mixed, w_out, preferred_element_type=jnp.float32)  14.6 us
    slice x2, local copies, waits for them, and re-layouts, attention_block(): values = projected[:, :, 2]  11.5 us

commit v1 on v0

--- a/solution.py
+++ b/solution.py
@@ -3,6 +3,8 @@
 import jax
 import jax.numpy as jnp
 from jax import lax
+from jax.experimental import pallas as pl
+from jax.experimental.pallas import tpu as pltpu
 from jax.sharding import PartitionSpec as P
 
 D = 512
@@ -74,7 +76,7 @@
     return result.astype(jnp.bfloat16).reshape(fine_tokens.shape)
 
 
-def body(
+def body_small(
     video,
     timestep,
     cond_weight,
@@ -133,26 +135,282 @@
     return result.reshape(frames_local, tokens_frame, features)
 
 
+CHUNKS = 2
+LOG2E = math.log2(math.e)
+ANY = pl.BlockSpec(memory_space=pl.ANY)
+VMEM = pl.BlockSpec(memory_space=pltpu.VMEM)
+
+
+def dot(a, b):
+    return jnp.dot(a, b, preferred_element_type=jnp.float32)
+
+
+def dot_t(a, b):
+    return lax.dot_general(a, b, (((1,), (1,)), ((), ())), preferred_element_type=jnp.float32)
+
+
+def normed_rows(x, gain, shift):
+    mean_square = jnp.mean(x * x, axis=-1, keepdims=True)
+    y = x * lax.rsqrt(mean_square + 1e-06) * gain
+    return (y if shift is None else y + shift).astype(jnp.bfloat16)
+
+
+def project(normed, w_ref, qkv_ref, width, step=512):
+    for i in range(0, 3 * width, step):
+        part = dot(normed, w_ref[:, i : i + step])
+        if i < width:
+            part = part * (LOG2E / math.sqrt(HEAD))
+        qkv_ref[:, i : i + step] = part.astype(jnp.bfloat16)
+
+
+def attend(qkv_ref, mixed_ref, width, bias, block):
+    rows = qkv_ref.shape[0]
+    low = lax.broadcasted_iota(jnp.int32, (1, 2 * HEAD), 1) < HEAD
+    for pair in range(width // (2 * HEAD)):
+        at = pair * 2 * HEAD
+        keys = qkv_ref[:, width + at : width + at + 2 * HEAD]
+        values = qkv_ref[:, 2 * width + at : 2 * width + at + 2 * HEAD]
+        zero = jnp.zeros_like(keys)
+        one = jnp.ones_like(keys)
+        sides = (
+            (jnp.where(low, keys, zero), jnp.where(low, values, one)),
+            (jnp.where(low, zero, keys), jnp.where(low, one, values)),
+        )
+        for r in range(0, rows, block):
+            queries = qkv_ref[r : r + block, at : at + 2 * HEAD]
+            got = []
+            for k_side, v_side in sides:
+                scores = dot_t(queries, k_side)
+                if bias is not None:
+                    scores = scores + bias
+                probs = jnp.exp2(scores - jnp.max(scores, axis=-1, keepdims=True))
+                got.append(dot(probs.astype(jnp.bfloat16), v_side))
+            top = jnp.where(low, got[0], got[1])
+            sums = pltpu.roll(jnp.where(low, got[1], got[0]), HEAD, 1)
+            mixed_ref[r : r + block, at : at + 2 * HEAD] = (top / sums).astype(jnp.bfloat16)
+
+
+def spatial_kernel(
+    n, x_ref, gain_ref, shift_ref, w_ref, wo_ref, *rest
+):
+    outs, (xs, xp, qkv, mixed) = rest[:-4], rest[-4:]
+    tokens, width = mixed.shape
+    cells = tokens // 4
+    part = cells // n // CHUNKS
+    for j in range(width // 128):
+        xs[j] = x_ref[0, :, j * 128 : (j + 1) * 128].astype(jnp.float32)
+        for q in range(4):
+            xp[q, :, j * 128 : (j + 1) * 128] = xs[j, pl.ds(q, cells, stride=4), :]
+    x = xp[...].reshape(tokens, width)
+    project(normed_rows(x, gain_ref[...], shift_ref[...]), w_ref, qkv, width)
+    attend(qkv, mixed, width, None, 256)
+    done = xp[...].reshape(tokens, width) + dot(mixed[...], wo_ref[...])
+    xp[...] = done.reshape(xp.shape)
+    for s in range(n):
+        for c in range(CHUNKS):
+            first = (s * CHUNKS + c) * part
+            outs[c][s] = xp[:, first : first + part, :].astype(jnp.bfloat16)
+
+
+def spatial_call(n, frame, video, gain, shift, w, wo):
+    _, tokens, width = video.shape
+    part = tokens // 4 // n // CHUNKS
+    return pl.pallas_call(
+        lambda *refs: spatial_kernel(n, *refs),
+        grid=(1,),
+        in_specs=[
+            pl.BlockSpec((1, tokens, width), lambda i: (frame, 0, 0)),
+            VMEM,
+            VMEM,
+            VMEM,
+            VMEM,
+        ],
+        out_specs=[VMEM] * CHUNKS,
+        out_shape=[jax.ShapeDtypeStruct((n, 4, part, width), jnp.bfloat16)] * CHUNKS,
+        scratch_shapes=[
+            pltpu.VMEM((width // 128, tokens, 128), jnp.float32),
+            pltpu.VMEM((4, tokens // 4, width), jnp.float32),
+            pltpu.VMEM((tokens, 3 * width), jnp.bfloat16),
+            pltpu.VMEM((tokens, width), jnp.bfloat16),
+        ],
+        cost_estimate=pl.CostEstimate(
+            flops=8 * tokens * width * width + 8 * tokens * tokens * width,
+            bytes_accessed=8 * width * width + 4 * tokens * width,
+            transcendentals=tokens * tokens * width // HEAD,
+        ),
+        name="spatial",
+    )(video, gain, shift, w, wo)
+
+
+def same_cell(rows, part):
+    a = lax.rem(lax.broadcasted_iota(jnp.int32, (rows, rows), 0), part)
+    b = lax.rem(lax.broadcasted_iota(jnp.int32, (rows, rows), 1), part)
+    return jnp.where(a == b, 0.0, -1e30).astype(jnp.float32)
+
+
+def window_kernel(n, frames, part, *refs):
+    pieces, refs = refs[:frames], refs[frames:]
+    gain, shift, coarse_gain, *hbm, out_ref = refs[:10]
+    xs, qkv, mixed, bias, cqkv, cmixed, *held, sems = refs[10:]
+    copies = [pltpu.make_async_copy(hbm[i], held[i], sems.at[i]) for i in range(6)]
+    for copy in copies:
+        copy.start()
+    wt, wto, wm, wc, wco, wu = held
+    rows, width = mixed.shape
+    coarse_rows, coarse_width = cmixed.shape
+    bias[...] = same_cell(rows, part)
+    for s in range(n):
+        for f in range(frames):
+            at = (s * frames + f) * part
+            for q in range(4):
+                xs[q, at : at + part, :] = pieces[f][s, q].astype(jnp.float32)
+    copies[0].wait()
+    copies[1].wait()
+
+    def temporal(q, carry):
+        project(normed_rows(xs[q], gain[...], shift[...]), wt, qkv, width)
+        attend(qkv, mixed, width, bias[...], rows)
+        fine = xs[q] + dot(mixed[...], wto[...])
+        xs[q] = fine.astype(jnp.bfloat16).astype(jnp.float32)
+        return carry
+
+    lax.fori_loop(0, 4, temporal, 0)
+    copies[2].wait()
+    coarse = None
+    for d in range(2):
+        for q in range(4):
+            fine = xs[q].reshape(coarse_rows // part, 2, part, width)[:, d]
+            fine = fine.reshape(coarse_rows, width).astype(jnp.bfloat16)
+            at = (d * 4 + q) * width
+            term = dot(fine, wm[at : at + width, :])
+            coarse = term if coarse is None else coarse + term
+    coarse = coarse.astype(jnp.bfloat16).astype(jnp.float32)
+    copies[3].wait()
+    project(normed_rows(coarse, coarse_gain[...], None), wc, cqkv, coarse_width)
+    attend(cqkv, cmixed, coarse_width, bias[:coarse_rows, :coarse_rows], coarse_rows)
+    copies[4].wait()
+    coarse = (coarse + dot(cmixed[...], wco[...])).astype(jnp.bfloat16)
+    copies[5].wait()
+    up = dot(coarse, wu[...])
+    for s in range(n):
+        for f in range(frames):
+            at = (s * frames + f) * part
+            pair = at // (2 * part) * part
+            for q in range(4):
+                done = xs[q, at : at + part, :] + up[pair : pair + part]
+                out_ref[s, f, q] = done.astype(jnp.bfloat16)
+
+
+def window_call(n, frames, pieces, vectors, weights):
+    part, width = pieces[0].shape[2:]
+    rows = n * frames * part
+    coarse_width = weights[3].shape[0]
+    flops = 2 * 4 * rows * (4 * width * width) + rows * 8 * width * coarse_width
+    flops += rows * (4 * coarse_width * coarse_width + coarse_width * width)
+    return pl.pallas_call(
+        lambda *refs: window_kernel(n, frames, part, *refs),
+        in_specs=[VMEM] * (frames + 3) + [ANY] * 6,
+        out_specs=VMEM,
+        out_shape=jax.ShapeDtypeStruct((n, frames, 4, part, width), jnp.bfloat16),
+        scratch_shapes=[
+            pltpu.VMEM((4, rows, width), jnp.float32),
+            pltpu.VMEM((rows, 3 * width), jnp.bfloat16),
+            pltpu.VMEM((rows, width), jnp.bfloat16),
+            pltpu.VMEM((rows, rows), jnp.float32),
+            pltpu.VMEM((rows // 2, 3 * coarse_width), jnp.bfloat16),
+            pltpu.VMEM((rows // 2, coarse_width), jnp.bfloat16),
+        ]
+        + [pltpu.VMEM(w.shape, w.dtype) for w in weights]
+        + [pltpu.SemaphoreType.DMA((6,))],
+        cost_estimate=pl.CostEstimate(
+            flops=flops,
+            bytes_accessed=sum(w.size for w in weights) * 2 + 16 * rows * width,
+            transcendentals=4 * rows * rows * width // HEAD,
+        ),
+        name="window",
+    )(*pieces, *vectors, *weights)
+
+
+def assemble_kernel(n, part, *refs):
+    pieces, out_ref, scratch = refs[:-2], refs[-2], refs[-1]
+    for s in range(n):
+        for c in range(CHUNKS):
+            first = (s * CHUNKS + c) * part * 4
+            for q in range(4):
+                rows = pieces[c][s, 0, q].astype(jnp.float32)
+                for j in range(scratch.shape[0]):
+                    block = rows[:, j * 128 : (j + 1) * 128]
+                    scratch[j, pl.ds(first + q, part, stride=4), :] = block
+    for j in range(scratch.shape[0]):
+        out_ref[0, :, j * 128 : (j + 1) * 128] = scratch[j].astype(jnp.bfloat16)
+
+
+def assemble_call(n, pieces, tokens):
+    _, frames, _, part, width = pieces[0].shape
+    return pl.pallas_call(
+        lambda *refs: assemble_kernel(n, part, *refs),
+        grid=(frames,),
+        in_specs=[pl.BlockSpec((n, 1, 4, part, width), lambda f: (0, f, 0, 0, 0))] * len(pieces),
+        out_specs=pl.BlockSpec((1, tokens, width), lambda f: (f, 0, 0)),
+        out_shape=jax.ShapeDtypeStruct((frames, tokens, width), jnp.bfloat16),
+        scratch_shapes=[pltpu.VMEM((width // 128, tokens, 128), jnp.float32)],
+        name="assemble",
+    )(*pieces)
+
+
+def body(
+    video,
+    timestep,
+    cond_weight,
+    spatial_gain,
+    spatial_qkv,
+    spatial_out,
+    temporal_gain,
+    temporal_qkv,
+    temporal_out,
+    merge_weight,
+    coarse_gain,
+    coarse_qkv,
+    coarse_out,
+    up_weight,
+):
+    frames, tokens, width = video.shape
+    n = lax.axis_size("frame")
+    modulation = modulation_of(timestep, cond_weight)
+    scale_s, shift_s, scale_t, shift_t = [
+        modulation[i * width : (i + 1) * width].reshape(1, width) for i in range(4)
+    ]
+    gain_s = spatial_gain.reshape(1, width) * (1.0 + scale_s)
+    gain_t = temporal_gain.reshape(1, width) * (1.0 + scale_t)
+
+    def exchange(array):
+        return lax.all_to_all(array, "frame", 0, 0, tiled=True)
+
+    landed = [
+        [exchange(a) for a in spatial_call(n, f, video, gain_s, shift_s, spatial_qkv, spatial_out)]
+        for f in range(frames)
+    ]
+    vectors = (gain_t, shift_t, coarse_gain.reshape(1, -1))
+    weights = (temporal_qkv, temporal_out, merge_weight, coarse_qkv, coarse_out, up_weight)
+    home = [
+        exchange(window_call(n, frames, [pair[c] for pair in landed], vectors, weights))
+        for c in range(CHUNKS)
+    ]
+    return assemble_call(n, home, tokens)
+
+
 def solution(mesh):
+    n = mesh.shape["frame"]
+    whole = P(("clip", "frame"), None, None)
+
+    def chosen(video, *rest):
+        tiled = video.shape[1] % (4 * n * CHUNKS * 8) == 0 and video.shape[0] % 2 == 0
+        return (body if tiled else body_small)(video, *rest)
+
     return jax.shard_map(
-        body,
+        chosen,
         mesh=mesh,
-        in_specs=(
-            P(("clip", "frame"), None, None),
-            P("clip"),
-            P(),
-            P(),
-            P(),
-            P(),
-            P(),
-            P(),
-            P(),
-            P(),
-            P(),
-            P(),
-            P(),
-            P(),
-        ),
-        out_specs=P(("clip", "frame"), None, None),
+        in_specs=(whole, P("clip")) + (P(),) * 12,
+        out_specs=whole,
         check_vma=False,
     )

time: 355 us -> 190 us (0.54); the launches traced: 348 us -> 189 us
  matrix products: 123 us -> 0.37 us
  local copies, waits for them, and re-layouts: 98 us -> 0.31 us
  Pallas kernels: 0 us -> 74.4 us
  blocking collectives: 107 us -> 87 us
  starting transfers between devices: 0 us -> 19.9 us
  other arithmetic: 18.8 us -> 1.37 us
  waiting for transfers between devices: 0 us -> 4.3 us
    dot_general x20 -> x0, matrix products: 87.6 us -> none  [the longest x6 30 us: attention_block(): jnp.dot(normed.reshape(length * batched, features), w_qkv, preferred_elem...]
    pallas_call x0 -> x7, Pallas kernels: none -> 74.4 us  [the longest x4 35.4 us: spatial_call(): pl.pallas_call(lambda *refs: spatial_kernel(n, *refs), grid=(1,), in_spec...]
    reshape x6 -> x0, local copies, waits for them, and re-layouts: 36.1 us -> none  [the longest x2 21.1 us: attention_block(): projected.astype(jnp.bfloat16)]
    sub x5 -> x0, matrix products: 33.7 us -> none  [attention_block(): probs = jax.nn.softmax(scores, axis=-1).astype(jnp.bfloat16)]
    convert_element_type x9 -> x0, local copies, waits for them, and re-layouts: 29.8 us -> none  [the longest x2 10.6 us: attention_block(): widened = inputs.astype(jnp.float32)]
    all_to_all x2 -> x5, blocking collectives: 107 us -> 87 us  [exchange(): return lax.all_to_all(array, 'frame', 0, 0, tiled=True)]
    all_to_all x0 -> x5, starting transfers between devices: none -> 19.9 us  [exchange(): return lax.all_to_all(array, 'frame', 0, 0, tiled=True)]
    slice x2 -> x0, local copies, waits for them, and re-layouts: 11.5 us -> none  [attention_block(): values = projected[:, :, 2]]
  transfers between devices with their start and end apart: 0 -> 5, of which waited for: 0 -> 1; matrix products, arithmetic and copies ran while one was open for 0% -> 0% of each run, Pallas kernels for 0% -> 33%
where the time goes in v1:
time: 190 us; the launch traced here: 189 us
  blocking collectives  87 us (46%)
  Pallas kernels  74.4 us (39%)
  starting transfers between devices  19.9 us (10%)
  waiting for transfers between devices  4.3 us (2%)
    all_to_all x5, blocking collectives, exchange(): return lax.all_to_all(array, 'frame', 0, 0, tiled=True)  87 us
    pallas_call x4, Pallas kernels, spatial_call(): pl.pallas_call(lambda *refs: spatial_kernel(n, *refs), grid=(1,), in_spec...  35.4 us
    pallas_call x2, Pallas kernels, window_call(): pl.pallas_call(lambda *refs: window_kernel(n, frames, part, *refs), in_sp...  35 us
    all_to_all x5, starting transfers between devices, exchange(): return lax.all_to_all(array, 'frame', 0, 0, tiled=True)  19.9 us
    all_to_all x5, waiting for transfers between devices, exchange(): return lax.all_to_all(array, 'frame', 0, 0, tiled=True)  4.3 us
    pallas_call x1, Pallas kernels, assemble_call(): pl.pallas_call(lambda *refs: assemble_kernel(n, part, *refs), grid=(frame...  3.98 us
  transfers between devices with their start and end apart: 5, of which 1 were waited for; matrix products, arithmetic and copies ran while one was open for 0% of the time, Pallas kernels for 33%

profile of v1, /device:TPU:0, one launch (start us, length us, event | category | flops | bytes accessed | tf_op | source)
XLA Modules:
  0.0 188.5 jit_solution(12303417028940951242)
XLA Ops:
  0.8 0.3 copy-done
  1.1 0.4 fusion.2
  1.4 1.3 fusion.8
  2.7 8.9 %spatial.7 = (bf16[8,4,8,512]{3,2,1,0:T(8,128)(2,1)}, bf16[8,4,8,512]{3,2,1,0:T(8,128)(2,1)}) custom-call(bf16[4,512,512]{2,1,0:T(8,128)(2,1)} %refs_0_.7, f32[1,512]{1,0:T(1,128)} %bitcast.22, f32[1,512]{1,0:T(1,128)} %bitcast.18, bf16[512,1536]{1,0:T(8,128)(2,1)} %refs_3_.7, bf16[512,512]{1,0:T(8,128)(2,1)} %refs_4_.7), custom_call_target="tpu_custom_call" | custom-call | flops 2147483648 | bytes 3145728 | tf_op jit(solution)/shard_map/spatial/pallas_call | solution.py:218
  11.6 16.3 %all_to_all.50.refs_3_ = bf16[8,4,8,512]{3,2,1,0:T(8,128)(2,1)} all-to-all(bf16[8,4,8,512]{3,2,1,0:T(8,128)(2,1)} %get-tuple-element.16), channel_id=1, replica_groups=mesh['clip'=4,'frame'=8] {'frame'}, dimensions={0} | all-to-all | bytes 524288 | tf_op jit(solution)/shard_map/all_to_all | solution.py:387
  27.9 3.6 %all-to-all-start.8 = ((bf16[8,4,8,512]{3,2,1,0:T(8,128)(2,1)}), bf16[8,4,8,512]{3,2,1,0:T(8,128)(2,1)S(1)}, u32[]{:S(2)}, u32[]{:S(2)}) async-start(bf16[8,4,8,512]{3,2,1,0:T(8,128)(2,1)} %get-tuple-element.20), calls=%async_computation.8 | async-start | bytes 524288 | tf_op jit(solution)/shard_map/all_to_all | solution.py:387
  31.5 8.9 %spatial.6 = (bf16[8,4,8,512]{3,2,1,0:T(8,128)(2,1)}, bf16[8,4,8,512]{3,2,1,0:T(8,128)(2,1)}) custom-call(bf16[4,512,512]{2,1,0:T(8,128)(2,1)} %refs_0_.7, f32[1,512]{1,0:T(1,128)} %bitcast.23, f32[1,512]{1,0:T(1,128)} %bitcast.19, bf16[512,1536]{1,0:T(8,128)(2,1)} %refs_3_.7, bf16[512,512]{1,0:T(8,128)(2,1)} %refs_4_.7), custom_call_target="tpu_custom_call" | custom-call | flops 2147483648 | bytes 3145728 | tf_op jit(solution)/shard_map/spatial/pallas_call | solution.py:218
  40.3 0.0 all-to-all-done.8.refs_3_
  40.4 14.3 %all_to_all.51.refs_2_ = bf16[8,4,8,512]{3,2,1,0:T(8,128)(2,1)} all-to-all(bf16[8,4,8,512]{3,2,1,0:T(8,128)(2,1)} %get-tuple-element.15), channel_id=1, replica_groups=mesh['clip'=4,'frame'=8] {'frame'}, dimensions={0} | all-to-all | bytes 524288 | tf_op jit(solution)/shard_map/all_to_all | solution.py:387
  54.7 3.6 %all-to-all-start.7 = ((bf16[8,4,8,512]{3,2,1,0:T(8,128)(2,1)}), bf16[8,4,8,512]{3,2,1,0:T(8,128)(2,1)S(1)}, u32[]{:S(2)}, u32[]{:S(2)}) async-start(bf16[8,4,8,512]{3,2,1,0:T(8,128)(2,1)} %get-tuple-element.19), calls=%async_computation.7 | async-start | bytes 524288 | tf_op jit(solution)/shard_map/all_to_all | solution.py:387
  58.3 8.8 %spatial.5 = (bf16[8,4,8,512]{3,2,1,0:T(8,128)(2,1)}, bf16[8,4,8,512]{3,2,1,0:T(8,128)(2,1)}) custom-call(bf16[4,512,512]{2,1,0:T(8,128)(2,1)} %refs_0_.7, f32[1,512]{1,0:T(1,128)} %bitcast.24, f32[1,512]{1,0:T(1,128)} %bitcast.20, bf16[512,1536]{1,0:T(8,128)(2,1)} %refs_3_.7, bf16[512,512]{1,0:T(8,128)(2,1)} %refs_4_.7), custom_call_target="tpu_custom_call" | custom-call | flops 2147483648 | bytes 3145728 | tf_op jit(solution)/shard_map/spatial/pallas_call | solution.py:218
  67.1 0.0 all-to-all-done.7.refs_2_
  67.1 14.1 %all_to_all.52.refs_1_ = bf16[8,4,8,512]{3,2,1,0:T(8,128)(2,1)} all-to-all(bf16[8,4,8,512]{3,2,1,0:T(8,128)(2,1)} %get-tuple-element.14), channel_id=1, replica_groups=mesh['clip'=4,'frame'=8] {'frame'}, dimensions={0} | all-to-all | bytes 524288 | tf_op jit(solution)/shard_map/all_to_all | solution.py:387
  81.2 3.4 %all-to-all-start.6 = ((bf16[8,4,8,512]{3,2,1,0:T(8,128)(2,1)}), bf16[8,4,8,512]{3,2,1,0:T(8,128)(2,1)S(1)}, u32[]{:S(2)}, u32[]{:S(2)}) async-start(bf16[8,4,8,512]{3,2,1,0:T(8,128)(2,1)} %get-tuple-element.18), calls=%async_computation.6 | async-start | bytes 524288 | tf_op jit(solution)/shard_map/all_to_all | solution.py:387
  84.6 8.9 %spatial.4 = (bf16[8,4,8,512]{3,2,1,0:T(8,128)(2,1)}, bf16[8,4,8,512]{3,2,1,0:T(8,128)(2,1)}) custom-call(bf16[4,512,512]{2,1,0:T(8,128)(2,1)} %refs_0_.7, f32[1,512]{1,0:T(1,128)} %bitcast.25, f32[1,512]{1,0:T(1,128)} %bitcast.21, bf16[512,1536]{1,0:T(8,128)(2,1)} %refs_3_.7, bf16[512,512]{1,0:T(8,128)(2,1)} %refs_4_.7), custom_call_target="tpu_custom_call" | custom-call | flops 2147483648 | bytes 3145728 | tf_op jit(solution)/shard_map/spatial/pallas_call | solution.py:218
  93.5 0.0 all-to-all-done.6.refs_1_
  93.5 14.3 %all_to_all.53.refs_0_ = bf16[8,4,8,512]{3,2,1,0:T(8,128)(2,1)} all-to-all(bf16[8,4,8,512]{3,2,1,0:T(8,128)(2,1)} %get-tuple-element.13), channel_id=1, replica_groups=mesh['clip'=4,'frame'=8] {'frame'}, dimensions={0} | all-to-all | bytes 524288 | tf_op jit(solution)/shard_map/all_to_all | solution.py:387
  107.8 3.6 %all-to-all-start.5 = ((bf16[8,4,8,512]{3,2,1,0:T(8,128)(2,1)}), bf16[8,4,8,512]{3,2,1,0:T(8,128)(2,1)S(1)}, u32[]{:S(2)}, u32[]{:S(2)}) async-start(bf16[8,4,8,512]{3,2,1,0:T(8,128)(2,1)} %get-tuple-element.17), calls=%async_computation.5 | async-start | bytes 524288 | tf_op jit(solution)/shard_map/all_to_all | solution.py:387
  111.4 17.5 %window.2 = bf16[8,4,4,8,512]{4,3,2,1,0:T(8,128)(2,1)} custom-call(bf16[8,4,8,512]{3,2,1,0:T(8,128)(2,1)} %all_to_all.53.refs_0_, bf16[8,4,8,512]{3,2,1,0:T(8,128)(2,1)} %all_to_all.52.refs_1_, bf16[8,4,8,512]{3,2,1,0:T(8,128)(2,1)} %all_to_all.51.refs_2_, bf16[8,4,8,512]{3,2,1,0:T(8,128)(2,1)} %all_to_all.50.refs_3_, f32[1,512]{1,0:T(1,128)} %bitcast.14, ...), custom_call_target="tpu_custom_call" | custom-call | flops 4429185024 | bytes 22020096 | tf_op jit(solution)/shard_map/window/pallas_call | solution.py:310
  129.0 5.7 %all-to-all-start.4 = ((bf16[8,4,4,8,512]{4,3,2,1,0:T(8,128)(2,1)}), bf16[8,4,4,8,512]{4,3,2,1,0:T(8,128)(2,1)S(1)}, u32[]{:S(2)}, u32[]{:S(2)}) async-start(bf16[8,4,4,8,512]{4,3,2,1,0:T(8,128)(2,1)} %window.2), calls=%async_computation.4 | async-start | bytes 2097152 | tf_op jit(solution)/shard_map/all_to_all | solution.py:387
  134.7 17.5 %window.3 = bf16[8,4,4,8,512]{4,3,2,1,0:T(8,128)(2,1)} custom-call(bf16[8,4,8,512]{3,2,1,0:T(8,128)(2,1)} %copy-done.5, bf16[8,4,8,512]{3,2,1,0:T(8,128)(2,1)} %copy-done.4, bf16[8,4,8,512]{3,2,1,0:T(8,128)(2,1)} %copy-done.3, bf16[8,4,8,512]{3,2,1,0:T(8,128)(2,1)} %copy-done.2, f32[1,512]{1,0:T(1,128)} %bitcast.15, f32[1,512]{1,0:T(1,128)} %bitcast.13, ...), custom_call_target="tpu_custom_call" | custom-call | flops 4429185024 | bytes 22020096 | tf_op jit(solution)/shard_map/window/pallas_call | solution.py:310
  152.2 4.3 %all-to-all-done.4.refs_0_ = bf16[8,4,4,8,512]{4,3,2,1,0:T(8,128)(2,1)S(1)} async-done(((bf16[8,4,4,8,512]{4,3,2,1,0:T(8,128)(2,1)}), bf16[8,4,4,8,512]{4,3,2,1,0:T(8,128)(2,1)S(1)}, u32[]{:S(2)}, u32[]{:S(2)}) %all-to-all-start.4) | async-done | bytes 1048608 | tf_op jit(solution)/shard_map/all_to_all | solution.py:387
  156.5 28.0 %all_to_all.54.refs_1_ = bf16[8,4,4,8,512]{4,3,2,1,0:T(8,128)(2,1)} all-to-all(bf16[8,4,4,8,512]{4,3,2,1,0:T(8,128)(2,1)} %window.3), channel_id=1, replica_groups=mesh['clip'=4,'frame'=8] {'frame'}, dimensions={0} | all-to-all | bytes 2097152 | tf_op jit(solution)/shard_map/all_to_all | solution.py:387
  184.5 4.0 %assemble.1 = bf16[4,512,512]{2,1,0:T(8,128)(2,1)} custom-call(bf16[8,4,4,8,512]{4,3,2,1,0:T(8,128)(2,1)} %copy-done.1, bf16[8,4,4,8,512]{4,3,2,1,0:T(8,128)(2,1)} %all_to_all.54.refs_1_), custom_call_target="tpu_custom_call" | custom-call | tf_op jit(solution)/shard_map/assemble/pallas_call | solution.py:350
  (13 shorter events, 0.1 us)
Async XLA Ops:
  0.0 1.1 copy-start
  27.9 12.5 %all-to-all-start.8 = ((bf16[8,4,8,512]{3,2,1,0:T(8,128)(2,1)}), bf16[8,4,8,512]{3,2,1,0:T(8,128)(2,1)S(1)}, u32[]{:S(2)}, u32[]{:S(2)}) async-start(bf16[8,4,8,512]{3,2,1,0:T(8,128)(2,1)} %get-tuple-element.20), calls=%async_computation.8 | async-start | bytes 524288 | tf_op jit(solution)/shard_map/all_to_all | solution.py:387
  40.3 26.8 %copy-start.2 = (bf16[8,4,8,512]{3,2,1,0:T(8,128)(2,1)}, bf16[8,4,8,512]{3,2,1,0:T(8,128)(2,1)S(1)}, u32[]{:S(2)}) copy-start(bf16[8,4,8,512]{3,2,1,0:T(8,128)(2,1)S(1)} %all-to-all-done.8.refs_3_) | copy-start | bytes 786436
  54.7 12.4 %all-to-all-start.7 = ((bf16[8,4,8,512]{3,2,1,0:T(8,128)(2,1)}), bf16[8,4,8,512]{3,2,1,0:T(8,128)(2,1)S(1)}, u32[]{:S(2)}, u32[]{:S(2)}) async-start(bf16[8,4,8,512]{3,2,1,0:T(8,128)(2,1)} %get-tuple-element.19), calls=%async_computation.7 | async-start | bytes 524288 | tf_op jit(solution)/shard_map/all_to_all | solution.py:387
  67.1 26.4 %copy-start.3 = (bf16[8,4,8,512]{3,2,1,0:T(8,128)(2,1)}, bf16[8,4,8,512]{3,2,1,0:T(8,128)(2,1)S(1)}, u32[]{:S(2)}) copy-start(bf16[8,4,8,512]{3,2,1,0:T(8,128)(2,1)S(1)} %all-to-all-done.7.refs_2_) | copy-start | bytes 786436
  81.2 12.3 %all-to-all-start.6 = ((bf16[8,4,8,512]{3,2,1,0:T(8,128)(2,1)}), bf16[8,4,8,512]{3,2,1,0:T(8,128)(2,1)S(1)}, u32[]{:S(2)}, u32[]{:S(2)}) async-start(bf16[8,4,8,512]{3,2,1,0:T(8,128)(2,1)} %get-tuple-element.18), calls=%async_computation.6 | async-start | bytes 524288 | tf_op jit(solution)/shard_map/all_to_all | solution.py:387
  93.5 35.4 %copy-start.4 = (bf16[8,4,8,512]{3,2,1,0:T(8,128)(2,1)}, bf16[8,4,8,512]{3,2,1,0:T(8,128)(2,1)S(1)}, u32[]{:S(2)}) copy-start(bf16[8,4,8,512]{3,2,1,0:T(8,128)(2,1)S(1)} %all-to-all-done.6.refs_1_) | copy-start | bytes 786436
  107.8 21.2 %all-to-all-start.5 = ((bf16[8,4,8,512]{3,2,1,0:T(8,128)(2,1)}), bf16[8,4,8,512]{3,2,1,0:T(8,128)(2,1)S(1)}, u32[]{:S(2)}, u32[]{:S(2)}) async-start(bf16[8,4,8,512]{3,2,1,0:T(8,128)(2,1)} %get-tuple-element.17), calls=%async_computation.5 | async-start | bytes 524288 | tf_op jit(solution)/shard_map/all_to_all | solution.py:387
  129.0 5.7 %copy-start.5 = (bf16[8,4,8,512]{3,2,1,0:T(8,128)(2,1)}, bf16[8,4,8,512]{3,2,1,0:T(8,128)(2,1)S(1)}, u32[]{:S(2)}) copy-start(bf16[8,4,8,512]{3,2,1,0:T(8,128)(2,1)S(1)} %all-to-all-done.5.refs_0_) | copy-start | bytes 786436
  129.0 27.5 %all-to-all-start.4 = ((bf16[8,4,4,8,512]{4,3,2,1,0:T(8,128)(2,1)}), bf16[8,4,4,8,512]{4,3,2,1,0:T(8,128)(2,1)S(1)}, u32[]{:S(2)}, u32[]{:S(2)}) async-start(bf16[8,4,4,8,512]{4,3,2,1,0:T(8,128)(2,1)} %window.2), calls=%async_computation.4 | async-start | bytes 2097152 | tf_op jit(solution)/shard_map/all_to_all | solution.py:387
  156.5 28.0 %copy-start.1 = (bf16[8,4,4,8,512]{4,3,2,1,0:T(8,128)(2,1)}, bf16[8,4,4,8,512]{4,3,2,1,0:T(8,128)(2,1)S(1)}, u32[]{:S(2)}) copy-start(bf16[8,4,4,8,512]{4,3,2,1,0:T(8,128)(2,1)S(1)} %all-to-all-done.4.refs_0_) | copy-start | bytes 3145732

commit v2 on v1

--- a/solution.py
+++ b/solution.py
@@ -209,24 +209,35 @@
     for s in range(n):
         for c in range(CHUNKS):
             first = (s * CHUNKS + c) * part
-            outs[c][s] = xp[:, first : first + part, :].astype(jnp.bfloat16)
-
-
-def spatial_call(n, frame, video, gain, shift, w, wo):
+            piece = xp[:, first : first + part, :].astype(jnp.bfloat16)
+            if len(outs) == 1:
+                outs[0][s, 0, c] = piece
+            else:
+                outs[c][s, 0] = piece
+
+
+def spatial_call(n, first, count, together, video, gain, shift, w, wo):
     _, tokens, width = video.shape
     part = tokens // 4 // n // CHUNKS
+    tail = (4, part, width)
+    if together:
+        out_shape = [jax.ShapeDtypeStruct((n, count, CHUNKS) + tail, jnp.bfloat16)]
+        out_specs = [pl.BlockSpec((n, 1, CHUNKS) + tail, lambda i: (0, i, 0, 0, 0, 0))]
+    else:
+        out_shape = [jax.ShapeDtypeStruct((n, count) + tail, jnp.bfloat16)] * CHUNKS
+        out_specs = [pl.BlockSpec((n, 1) + tail, lambda i: (0, i, 0, 0, 0))] * CHUNKS
     return pl.pallas_call(
         lambda *refs: spatial_kernel(n, *refs),
-        grid=(1,),
+        grid=(count,),
         in_specs=[
-            pl.BlockSpec((1, tokens, width), lambda i: (frame, 0, 0)),
+            pl.BlockSpec((1, tokens, width), lambda i: (first + i, 0, 0)),
             VMEM,
             VMEM,
             VMEM,
             VMEM,
         ],
-        out_specs=[VMEM] * CHUNKS,
-        out_shape=[jax.ShapeDtypeStruct((n, 4, part, width), jnp.bfloat16)] * CHUNKS,
+        out_specs=out_specs,
+        out_shape=out_shape,
         scratch_shapes=[
             pltpu.VMEM((width // 128, tokens, 128), jnp.float32),
             pltpu.VMEM((4, tokens // 4, width), jnp.float32),
@@ -234,9 +245,9 @@
             pltpu.VMEM((tokens, width), jnp.bfloat16),
         ],
         cost_estimate=pl.CostEstimate(
-            flops=8 * tokens * width * width + 8 * tokens * tokens * width,
-            bytes_accessed=8 * width * width + 4 * tokens * width,
-            transcendentals=tokens * tokens * width // HEAD,
+            flops=count * (8 * tokens * width * width + 8 * tokens * tokens * width),
+            bytes_accessed=8 * width * width + count * 4 * tokens * width,
+            transcendentals=count * tokens * tokens * width // HEAD,
         ),
         name="spatial",
     )(video, gain, shift, w, wo)
@@ -248,8 +259,8 @@
     return jnp.where(a == b, 0.0, -1e30).astype(jnp.float32)
 
 
-def window_kernel(n, frames, part, *refs):
-    pieces, refs = refs[:frames], refs[frames:]
+def window_kernel(n, frames, part, groups, *refs):
+    pieces, refs = refs[:groups], refs[groups:]
     gain, shift, coarse_gain, *hbm, out_ref = refs[:10]
     xs, qkv, mixed, bias, cqkv, cmixed, *held, sems = refs[10:]
     copies = [pltpu.make_async_copy(hbm[i], held[i], sems.at[i]) for i in range(6)]
@@ -262,8 +273,11 @@
     for s in range(n):
         for f in range(frames):
             at = (s * frames + f) * part
+            g, i = divmod(f, frames // groups)
+            piece = pieces[g]
             for q in range(4):
-                xs[q, at : at + part, :] = pieces[f][s, q].astype(jnp.float32)
+                rows_q = piece[s, i, 0, q] if len(piece.shape) == 6 else piece[s, i, q]
+                xs[q, at : at + part, :] = rows_q.astype(jnp.float32)
     copies[0].wait()
     copies[1].wait()
 
@@ -301,15 +315,23 @@
                 out_ref[s, f, q] = done.astype(jnp.bfloat16)
 
 
-def window_call(n, frames, pieces, vectors, weights):
-    part, width = pieces[0].shape[2:]
+def window_call(n, frames, chunk, pieces, vectors, weights):
+    part, width = pieces[0].shape[-2:]
+
+    def spec(a):
+        if a.ndim == 5:
+            return VMEM
+        shape = a.shape[:2] + (1,) + a.shape[3:]
+        return pl.BlockSpec(shape, lambda i: (0, 0, chunk, 0, 0, 0))
+
     rows = n * frames * part
     coarse_width = weights[3].shape[0]
     flops = 2 * 4 * rows * (4 * width * width) + rows * 8 * width * coarse_width
     flops += rows * (4 * coarse_width * coarse_width + coarse_width * width)
     return pl.pallas_call(
-        lambda *refs: window_kernel(n, frames, part, *refs),
-        in_specs=[VMEM] * (frames + 3) + [ANY] * 6,
+        lambda *refs: window_kernel(n, frames, part, len(pieces), *refs),
+        grid=(1,),
+        in_specs=[spec(a) for a in pieces] + [VMEM] * 3 + [ANY] * 6,
         out_specs=VMEM,
         out_shape=jax.ShapeDtypeStruct((n, frames, 4, part, width), jnp.bfloat16),
         scratch_shapes=[
@@ -386,14 +408,14 @@
     def exchange(array):
         return lax.all_to_all(array, "frame", 0, 0, tiled=True)
 
-    landed = [
-        [exchange(a) for a in spatial_call(n, f, video, gain_s, shift_s, spatial_qkv, spatial_out)]
-        for f in range(frames)
-    ]
+    block = (video, gain_s, shift_s, spatial_qkv, spatial_out)
+    half = frames // 2
+    early = [exchange(a) for a in spatial_call(n, 0, half, True, *block)]
+    late = [exchange(a) for a in spatial_call(n, half, frames - half, False, *block)]
     vectors = (gain_t, shift_t, coarse_gain.reshape(1, -1))
     weights = (temporal_qkv, temporal_out, merge_weight, coarse_qkv, coarse_out, up_weight)
     home = [
-        exchange(window_call(n, frames, [pair[c] for pair in landed], vectors, weights))
+        exchange(window_call(n, frames, c, [early[0], late[c]], vectors, weights))
         for c in range(CHUNKS)
     ]
     return assemble_call(n, home, tokens)

time: 190 us -> 158 us (0.83)
  blocking collectives: 87 us -> 60.8 us
  Pallas kernels: 74.4 us -> 69.7 us
  waiting for transfers between devices: 4.3 us -> 7.47 us
  starting transfers between devices: 19.9 us -> 16.8 us
    all_to_all x5 -> x2, blocking collectives: 87 us -> 60.8 us  [exchange(): return lax.all_to_all(array, 'frame', 0, 0, tiled=True)]
    pallas_call x6 -> x4, Pallas kernels: 70.4 us -> 65.8 us  [the longest x2 35 us: window_call(): pl.pallas_call(lambda *refs: window_kernel(n, frames, part, len(pieces),...]
    all_to_all x5 -> x3, waiting for transfers between devices: 4.3 us -> 7.47 us  [exchange(): return lax.all_to_all(array, 'frame', 0, 0, tiled=True)]
    all_to_all x5 -> x3, starting transfers between devices: 19.9 us -> 16.8 us  [exchange(): return lax.all_to_all(array, 'frame', 0, 0, tiled=True)]
  transfers between devices with their start and end apart: 5 -> 3, of which waited for: 1 -> 1; matrix products, arithmetic and copies ran while one was open for 0% -> 0% of each run, Pallas kernels for 33% -> 32%
where the time goes in v2:
time: 158 us
  Pallas kernels  69.7 us (44%)
  blocking collectives  60.8 us (38%)
  starting transfers between devices  16.8 us (11%)
  waiting for transfers between devices  7.47 us (5%)
    all_to_all x2, blocking collectives, exchange(): return lax.all_to_all(array, 'frame', 0, 0, tiled=True)  60.8 us
    pallas_call x2, Pallas kernels, window_call(): pl.pallas_call(lambda *refs: window_kernel(n, frames, part, len(pieces),...  35 us
    pallas_call x2, Pallas kernels, spatial_call(): pl.pallas_call(lambda *refs: spatial_kernel(n, *refs), grid=(count,), in_...  30.7 us
    all_to_all x3, starting transfers between devices, exchange(): return lax.all_to_all(array, 'frame', 0, 0, tiled=True)  16.8 us
    all_to_all x3, waiting for transfers between devices, exchange(): return lax.all_to_all(array, 'frame', 0, 0, tiled=True)  7.47 us
    pallas_call x1, Pallas kernels, assemble_call(): pl.pallas_call(lambda *refs: assemble_kernel(n, part, *refs), grid=(frame...  3.98 us
  transfers between devices with their start and end apart: 3, of which 1 were waited for; matrix products, arithmetic and copies ran while one was open for 0% of the time, Pallas kernels for 32%

profile of v2, /device:TPU:0, one launch (start us, length us, event | category | flops | bytes accessed | tf_op | source)
XLA Modules:
  0.0 157.6 jit_solution(11186339177535184815)
XLA Ops:
  0.0 0.0 copy-start
  0.8 0.3 copy-done
  1.1 0.4 fusion.2
  1.4 1.3 fusion.8
  2.7 15.3 %spatial.3 = (bf16[8,2,4,8,512]{4,3,2,1,0:T(8,128)(2,1)}, bf16[8,2,4,8,512]{4,3,2,1,0:T(8,128)(2,1)}) custom-call(bf16[4,512,512]{2,1,0:T(8,128)(2,1)} %refs_0_.3, f32[1,512]{1,0:T(1,128)} %bitcast.20, f32[1,512]{1,0:T(1,128)} %bitcast.18, bf16[512,1536]{1,0:T(8,128)(2,1)} %refs_3_.3, bf16[512,512]{1,0:T(8,128)(2,1)} %refs_4_.3), custom_call_target="tpu_custom_call" | custom-call | flops 4294967296 | bytes 4194304 | tf_op jit(solution)/shard_map/spatial/pallas_call | solution.py:229
  18.1 7.3 %all-to-all-start.1 = ((bf16[8,2,4,8,512]{4,3,2,1,0:T(8,128)(2,1)}), bf16[8,2,4,8,512]{4,3,2,1,0:T(8,128)(2,1)S(1)}, u32[]{:S(2)}, u32[]{:S(2)}) async-start(bf16[8,2,4,8,512]{4,3,2,1,0:T(8,128)(2,1)} %get-tuple-element.7), calls=%async_computation.1 | async-start | bytes 1048576 | tf_op jit(solution)/shard_map/all_to_all | solution.py:409
  25.4 15.4 %spatial.2 = bf16[8,2,2,4,8,512]{5,4,3,2,1,0:T(8,128)(2,1)} custom-call(bf16[4,512,512]{2,1,0:T(8,128)(2,1)} %refs_0_.3, f32[1,512]{1,0:T(1,128)} %bitcast.21, f32[1,512]{1,0:T(1,128)} %bitcast.19, bf16[512,1536]{1,0:T(8,128)(2,1)} %refs_3_.3, bf16[512,512]{1,0:T(8,128)(2,1)} %refs_4_.3), custom_call_target="tpu_custom_call" | custom-call | flops 4294967296 | bytes 4194304 | tf_op jit(solution)/shard_map/spatial/pallas_call | solution.py:229
  40.8 0.0 all-to-all-done.1.refs_1_
  40.8 0.0 copy-start.2
  40.8 31.3 %all_to_all.25.refs_0_ = bf16[8,2,2,4,8,512]{5,4,3,2,1,0:T(8,128)(2,1)} all-to-all(bf16[8,2,2,4,8,512]{5,4,3,2,1,0:T(8,128)(2,1)} %spatial.2), channel_id=1, replica_groups=mesh['clip'=4,'frame'=8] {'frame'}, dimensions={0} | all-to-all | bytes 2097152 | tf_op jit(solution)/shard_map/all_to_all | solution.py:409
  72.1 3.7 %all-to-all-start.3 = ((bf16[8,2,4,8,512]{4,3,2,1,0:T(8,128)(2,1)}), bf16[8,2,4,8,512]{4,3,2,1,0:T(8,128)(2,1)S(1)}, u32[]{:S(2)}, u32[]{:S(2)}) async-start(bf16[8,2,4,8,512]{4,3,2,1,0:T(8,128)(2,1)} %get-tuple-element.8), calls=%async_computation.3 | async-start | bytes 1048576 | tf_op jit(solution)/shard_map/all_to_all | solution.py:409
  75.8 0.0 copy-done.2
  75.8 17.5 %window.2 = bf16[8,4,4,8,512]{4,3,2,1,0:T(8,128)(2,1)} custom-call(bf16[8,2,2,4,8,512]{5,4,3,2,1,0:T(8,128)(2,1)} %all_to_all.25.refs_0_, bf16[8,2,4,8,512]{4,3,2,1,0:T(8,128)(2,1)} %copy-done.2, f32[1,512]{1,0:T(1,128)} %bitcast.14, f32[1,512]{1,0:T(1,128)} %bitcast.12, f32[1,1024]{1,0:T(1,128)} %bitcast.16, bf16[512,1536]{1,0:T(8,128)(2,1)} %refs_5_.3, ...), custom_call_target="tpu_custom_call" | custom-call | flops 4429185024 | bytes 22020096 | tf_op jit(solution)/shard_map/window/pallas_call | solution.py:331
  93.3 0.0 all-to-all-done.3.refs_1_
  93.3 0.0 copy-start.3
  93.3 5.9 %all-to-all-start.2 = ((bf16[8,4,4,8,512]{4,3,2,1,0:T(8,128)(2,1)}), bf16[8,4,4,8,512]{4,3,2,1,0:T(8,128)(2,1)S(1)}, u32[]{:S(2)}, u32[]{:S(2)}) async-start(bf16[8,4,4,8,512]{4,3,2,1,0:T(8,128)(2,1)} %window.2), calls=%async_computation.2 | async-start | bytes 2097152 | tf_op jit(solution)/shard_map/all_to_all | solution.py:409
  99.2 0.0 copy-done.3
  99.2 17.5 %window.3 = bf16[8,4,4,8,512]{4,3,2,1,0:T(8,128)(2,1)} custom-call(bf16[8,2,2,4,8,512]{5,4,3,2,1,0:T(8,128)(2,1)} %all_to_all.25.refs_0_, bf16[8,2,4,8,512]{4,3,2,1,0:T(8,128)(2,1)} %copy-done.3, f32[1,512]{1,0:T(1,128)} %bitcast.15, f32[1,512]{1,0:T(1,128)} %bitcast.13, f32[1,1024]{1,0:T(1,128)} %bitcast.17, bf16[512,1536]{1,0:T(8,128)(2,1)} %refs_5_.3, ...), custom_call_target="tpu_custom_call" | custom-call | flops 4429185024 | bytes 22020096 | tf_op jit(solution)/shard_map/window/pallas_call | solution.py:331
  116.7 7.5 %all-to-all-done.2.refs_0_ = bf16[8,4,4,8,512]{4,3,2,1,0:T(8,128)(2,1)S(1)} async-done(((bf16[8,4,4,8,512]{4,3,2,1,0:T(8,128)(2,1)}), bf16[8,4,4,8,512]{4,3,2,1,0:T(8,128)(2,1)S(1)}, u32[]{:S(2)}, u32[]{:S(2)}) %all-to-all-start.2) | async-done | bytes 1048608 | tf_op jit(solution)/shard_map/all_to_all | solution.py:409
  124.2 0.0 copy-start.1
  124.2 29.5 %all_to_all.26.refs_1_ = bf16[8,4,4,8,512]{4,3,2,1,0:T(8,128)(2,1)} all-to-all(bf16[8,4,4,8,512]{4,3,2,1,0:T(8,128)(2,1)} %window.3), channel_id=1, replica_groups=mesh['clip'=4,'frame'=8] {'frame'}, dimensions={0} | all-to-all | bytes 2097152 | tf_op jit(solution)/shard_map/all_to_all | solution.py:409
  153.7 0.0 copy-done.1
  153.7 4.0 %assemble.1 = bf16[4,512,512]{2,1,0:T(8,128)(2,1)} custom-call(bf16[8,4,4,8,512]{4,3,2,1,0:T(8,128)(2,1)} %copy-done.1, bf16[8,4,4,8,512]{4,3,2,1,0:T(8,128)(2,1)} %all_to_all.26.refs_1_), custom_call_target="tpu_custom_call" | custom-call | tf_op jit(solution)/shard_map/assemble/pallas_call | solution.py:372
  (1 shorter events, 0.0 us)
Async XLA Ops:
  0.0 1.1 copy-start
  18.1 22.7 %all-to-all-start.1 = ((bf16[8,2,4,8,512]{4,3,2,1,0:T(8,128)(2,1)}), bf16[8,2,4,8,512]{4,3,2,1,0:T(8,128)(2,1)S(1)}, u32[]{:S(2)}, u32[]{:S(2)}) async-start(bf16[8,2,4,8,512]{4,3,2,1,0:T(8,128)(2,1)} %get-tuple-element.7), calls=%async_computation.1 | async-start | bytes 1048576 | tf_op jit(solution)/shard_map/all_to_all | solution.py:409
  40.8 35.0 %copy-start.2 = (bf16[8,2,4,8,512]{4,3,2,1,0:T(8,128)(2,1)}, bf16[8,2,4,8,512]{4,3,2,1,0:T(8,128)(2,1)S(1)}, u32[]{:S(2)}) copy-start(bf16[8,2,4,8,512]{4,3,2,1,0:T(8,128)(2,1)S(1)} %all-to-all-done.1.refs_1_) | copy-start | bytes 1572868
  72.1 21.2 %all-to-all-start.3 = ((bf16[8,2,4,8,512]{4,3,2,1,0:T(8,128)(2,1)}), bf16[8,2,4,8,512]{4,3,2,1,0:T(8,128)(2,1)S(1)}, u32[]{:S(2)}, u32[]{:S(2)}) async-start(bf16[8,2,4,8,512]{4,3,2,1,0:T(8,128)(2,1)} %get-tuple-element.8), calls=%async_computation.3 | async-start | bytes 1048576 | tf_op jit(solution)/shard_map/all_to_all | solution.py:409
  93.3 5.9 %copy-start.3 = (bf16[8,2,4,8,512]{4,3,2,1,0:T(8,128)(2,1)}, bf16[8,2,4,8,512]{4,3,2,1,0:T(8,128)(2,1)S(1)}, u32[]{:S(2)}) copy-start(bf16[8,2,4,8,512]{4,3,2,1,0:T(8,128)(2,1)S(1)} %all-to-all-done.3.refs_1_) | copy-start | bytes 1572868
  93.3 30.9 %all-to-all-start.2 = ((bf16[8,4,4,8,512]{4,3,2,1,0:T(8,128)(2,1)}), bf16[8,4,4,8,512]{4,3,2,1,0:T(8,128)(2,1)S(1)}, u32[]{:S(2)}, u32[]{:S(2)}) async-start(bf16[8,4,4,8,512]{4,3,2,1,0:T(8,128)(2,1)} %window.2), calls=%async_computation.2 | async-start | bytes 2097152 | tf_op jit(solution)/shard_map/all_to_all | solution.py:409
  124.2 29.5 %copy-start.1 = (bf16[8,4,4,8,512]{4,3,2,1,0:T(8,128)(2,1)}, bf16[8,4,4,8,512]{4,3,2,1,0:T(8,128)(2,1)S(1)}, u32[]{:S(2)}) copy-start(bf16[8,4,4,8,512]{4,3,2,1,0:T(8,128)(2,1)S(1)} %all-to-all-done.2.refs_0_) | copy-start | bytes 3145732

commit v3 on v2

--- a/solution.py
+++ b/solution.py
@@ -190,10 +190,8 @@
             mixed_ref[r : r + block, at : at + 2 * HEAD] = (top / sums).astype(jnp.bfloat16)
 
 
-def spatial_kernel(
-    n, x_ref, gain_ref, shift_ref, w_ref, wo_ref, *rest
-):
-    outs, (xs, xp, qkv, mixed) = rest[:-4], rest[-4:]
+def spatial_kernel(n, x_ref, gain_ref, shift_ref, w_ref, wo_ref, *rest):
+    outs, (xs, xp, qkv, mixed) = rest[-4 - CHUNKS : -4], rest[-4:]
     tokens, width = mixed.shape
     cells = tokens // 4
     part = cells // n // CHUNKS
@@ -209,23 +207,13 @@
     for s in range(n):
         for c in range(CHUNKS):
             first = (s * CHUNKS + c) * part
-            piece = xp[:, first : first + part, :].astype(jnp.bfloat16)
-            if len(outs) == 1:
-                outs[0][s, 0, c] = piece
-            else:
-                outs[c][s, 0] = piece
-
-
-def spatial_call(n, first, count, together, video, gain, shift, w, wo):
-    _, tokens, width = video.shape
-    part = tokens // 4 // n // CHUNKS
-    tail = (4, part, width)
-    if together:
-        out_shape = [jax.ShapeDtypeStruct((n, count, CHUNKS) + tail, jnp.bfloat16)]
-        out_specs = [pl.BlockSpec((n, 1, CHUNKS) + tail, lambda i: (0, i, 0, 0, 0, 0))]
-    else:
-        out_shape = [jax.ShapeDtypeStruct((n, count) + tail, jnp.bfloat16)] * CHUNKS
-        out_specs = [pl.BlockSpec((n, 1) + tail, lambda i: (0, i, 0, 0, 0))] * CHUNKS
+            outs[c][s, 0] = xp[:, first : first + part, :].astype(jnp.bfloat16)
+
+
+def spatial_call(n, first, count, rest, video, gain, shift, w, wo):
+    frames, tokens, width = video.shape
+    tail = (4, tokens // 4 // n // CHUNKS, width)
+    taken = [] if rest is None else [rest]
     return pl.pallas_call(
         lambda *refs: spatial_kernel(n, *refs),
         grid=(count,),
@@ -235,9 +223,17 @@
             VMEM,
             VMEM,
             VMEM,
+        ]
+        + [ANY] * len(taken),
+        out_specs=[
+            pl.BlockSpec((n, 1) + tail, lambda i: (0, i, 0, 0, 0)),
+            pl.BlockSpec((n, 1) + tail, lambda i: (0, first + i, 0, 0, 0)),
         ],
-        out_specs=out_specs,
-        out_shape=out_shape,
+        out_shape=[
+            jax.ShapeDtypeStruct((n, count) + tail, jnp.bfloat16),
+            jax.ShapeDtypeStruct((n, frames) + tail, jnp.bfloat16),
+        ],
+        input_output_aliases={5: 1} if taken else {},
         scratch_shapes=[
             pltpu.VMEM((width // 128, tokens, 128), jnp.float32),
             pltpu.VMEM((4, tokens // 4, width), jnp.float32),
@@ -250,7 +246,7 @@
             transcendentals=count * tokens * tokens * width // HEAD,
         ),
         name="spatial",
-    )(video, gain, shift, w, wo)
+    )(video, gain, shift, w, wo, *taken)
 
 
 def same_cell(rows, part):
@@ -262,7 +258,7 @@
 def window_kernel(n, frames, part, groups, *refs):
     pieces, refs = refs[:groups], refs[groups:]
     gain, shift, coarse_gain, *hbm, out_ref = refs[:10]
-    xs, qkv, mixed, bias, cqkv, cmixed, *held, sems = refs[10:]
+    xs, qkv, mixed, bias, cqkv, cmixed, ordered, *held, sems = refs[10:]
     copies = [pltpu.make_async_copy(hbm[i], held[i], sems.at[i]) for i in range(6)]
     for copy in copies:
         copy.start()
@@ -274,10 +270,8 @@
         for f in range(frames):
             at = (s * frames + f) * part
             g, i = divmod(f, frames // groups)
-            piece = pieces[g]
             for q in range(4):
-                rows_q = piece[s, i, 0, q] if len(piece.shape) == 6 else piece[s, i, q]
-                xs[q, at : at + part, :] = rows_q.astype(jnp.float32)
+                xs[q, at : at + part, :] = pieces[g][s, i, q].astype(jnp.float32)
     copies[0].wait()
     copies[1].wait()
 
@@ -312,28 +306,28 @@
             pair = at // (2 * part) * part
             for q in range(4):
                 done = xs[q, at : at + part, :] + up[pair : pair + part]
-                out_ref[s, f, q] = done.astype(jnp.bfloat16)
-
-
-def window_call(n, frames, chunk, pieces, vectors, weights):
+                for j in range(width // 128):
+                    lanes = done[:, j * 128 : (j + 1) * 128]
+                    ordered[j, pl.ds(4 * at + q, part, stride=4), :] = lanes
+    for s in range(n):
+        for f in range(frames):
+            at = (s * frames + f) * part * 4
+            for j in range(width // 128):
+                lanes = ordered[j, at : at + 4 * part, :]
+                out_ref[s, f, :, j * 128 : (j + 1) * 128] = lanes.astype(jnp.bfloat16)
+
+
+def window_call(n, frames, pieces, vectors, weights):
     part, width = pieces[0].shape[-2:]
-
-    def spec(a):
-        if a.ndim == 5:
-            return VMEM
-        shape = a.shape[:2] + (1,) + a.shape[3:]
-        return pl.BlockSpec(shape, lambda i: (0, 0, chunk, 0, 0, 0))
-
     rows = n * frames * part
     coarse_width = weights[3].shape[0]
     flops = 2 * 4 * rows * (4 * width * width) + rows * 8 * width * coarse_width
     flops += rows * (4 * coarse_width * coarse_width + coarse_width * width)
     return pl.pallas_call(
         lambda *refs: window_kernel(n, frames, part, len(pieces), *refs),
-        grid=(1,),
-        in_specs=[spec(a) for a in pieces] + [VMEM] * 3 + [ANY] * 6,
+        in_specs=[VMEM] * (len(pieces) + 3) + [ANY] * 6,
         out_specs=VMEM,
-        out_shape=jax.ShapeDtypeStruct((n, frames, 4, part, width), jnp.bfloat16),
+        out_shape=jax.ShapeDtypeStruct((n, frames, 4 * part, width), jnp.bfloat16),
         scratch_shapes=[
             pltpu.VMEM((4, rows, width), jnp.float32),
             pltpu.VMEM((rows, 3 * width), jnp.bfloat16),
@@ -341,6 +335,7 @@
             pltpu.VMEM((rows, rows), jnp.float32),
             pltpu.VMEM((rows // 2, 3 * coarse_width), jnp.bfloat16),
             pltpu.VMEM((rows // 2, coarse_width), jnp.bfloat16),
+            pltpu.VMEM((width // 128, 4 * rows, 128), jnp.float32),
         ]
         + [pltpu.VMEM(w.shape, w.dtype) for w in weights]
         + [pltpu.SemaphoreType.DMA((6,))],
@@ -353,31 +348,25 @@
     )(*pieces, *vectors, *weights)
 
 
-def assemble_kernel(n, part, *refs):
-    pieces, out_ref, scratch = refs[:-2], refs[-2], refs[-1]
-    for s in range(n):
-        for c in range(CHUNKS):
-            first = (s * CHUNKS + c) * part * 4
-            for q in range(4):
-                rows = pieces[c][s, 0, q].astype(jnp.float32)
-                for j in range(scratch.shape[0]):
-                    block = rows[:, j * 128 : (j + 1) * 128]
-                    scratch[j, pl.ds(first + q, part, stride=4), :] = block
-    for j in range(scratch.shape[0]):
-        out_ref[0, :, j * 128 : (j + 1) * 128] = scratch[j].astype(jnp.bfloat16)
-
-
-def assemble_call(n, pieces, tokens):
-    _, frames, _, part, width = pieces[0].shape
+def place_kernel(piece_ref, *refs):
+    refs[-1][0, :, 0] = piece_ref[:, 0]
+
+
+def place_call(chunk, piece, result):
+    n, frames, rows, width = piece.shape
+    taken = [] if result is None else [result]
     return pl.pallas_call(
-        lambda *refs: assemble_kernel(n, part, *refs),
+        place_kernel,
         grid=(frames,),
-        in_specs=[pl.BlockSpec((n, 1, 4, part, width), lambda f: (0, f, 0, 0, 0))] * len(pieces),
-        out_specs=pl.BlockSpec((1, tokens, width), lambda f: (f, 0, 0)),
-        out_shape=jax.ShapeDtypeStruct((frames, tokens, width), jnp.bfloat16),
-        scratch_shapes=[pltpu.VMEM((width // 128, tokens, 128), jnp.float32)],
-        name="assemble",
-    )(*pieces)
+        in_specs=[pl.BlockSpec((n, 1, rows, width), lambda f: (0, f, 0, 0))] + [ANY] * len(taken),
+        out_specs=pl.BlockSpec((1, n, 1, rows, width), lambda f: (f, 0, chunk, 0, 0)),
+        out_shape=jax.ShapeDtypeStruct((frames, n, CHUNKS, rows, width), jnp.bfloat16),
+        input_output_aliases={1: 0} if taken else {},
+        cost_estimate=pl.CostEstimate(
+            flops=0, bytes_accessed=4 * piece.size, transcendentals=0
+        ),
+        name="place",
+    )(piece, *taken)
 
 
 def body(
@@ -410,23 +399,29 @@
 
     block = (video, gain_s, shift_s, spatial_qkv, spatial_out)
     half = frames // 2
-    early = [exchange(a) for a in spatial_call(n, 0, half, True, *block)]
-    late = [exchange(a) for a in spatial_call(n, half, frames - half, False, *block)]
+    early, rest = spatial_call(n, 0, half, None, *block)
+    early = exchange(early)
+    late, rest = spatial_call(n, half, frames - half, rest, *block)
+    late = exchange(late)
+    rest = exchange(rest)
     vectors = (gain_t, shift_t, coarse_gain.reshape(1, -1))
     weights = (temporal_qkv, temporal_out, merge_weight, coarse_qkv, coarse_out, up_weight)
-    home = [
-        exchange(window_call(n, frames, c, [early[0], late[c]], vectors, weights))
-        for c in range(CHUNKS)
-    ]
-    return assemble_call(n, home, tokens)
+    home = []
+    for pieces in ((early, late), (rest,)):
+        part = window_call(n, frames, pieces, vectors, weights)
+        home.append(exchange(part))
+    result = None
+    for c in range(CHUNKS):
+        result = place_call(c, home[c], result)
+    return result.reshape(frames, tokens, width)
 
 
 def solution(mesh):
-    n = mesh.shape["frame"]
     whole = P(("clip", "frame"), None, None)
 
     def chosen(video, *rest):
-        tiled = video.shape[1] % (4 * n * CHUNKS * 8) == 0 and video.shape[0] % 2 == 0
+        n = mesh.shape["frame"]
+        tiled = video.shape[1] % (4 * n * CHUNKS * 8) == 0 and video.shape[0] % 4 == 0
         return (body if tiled else body_small)(video, *rest)
 
     return jax.shard_map(

time: 158 us -> 154 us (0.975)
  blocking collectives: 60.8 us -> 20.1 us
  waiting for transfers between devices: 7.47 us -> 38.3 us
  Pallas kernels: 69.7 us -> 72.9 us
    all_to_all x2 -> x1, blocking collectives: 60.8 us -> 20.1 us  [exchange(): return lax.all_to_all(array, 'frame', 0, 0, tiled=True)]
    all_to_all x3 -> x4, waiting for transfers between devices: 7.47 us -> 38.3 us  [exchange(): return lax.all_to_all(array, 'frame', 0, 0, tiled=True)]
    pallas_call x1 -> x2, Pallas kernels: 3.98 us -> 6.73 us  [place_call(): pl.pallas_call(place_kernel, grid=(frames,), in_specs=[pl.BlockSpec((n, 1...]
    all_to_all x3 -> x4, starting transfers between devices: 16.8 us -> 18.2 us  [exchange(): return lax.all_to_all(array, 'frame', 0, 0, tiled=True)]
  transfers between devices with their start and end apart: 3 -> 4, of which waited for: 1 -> 3; matrix products, arithmetic and copies ran while one was open for 0% -> 0% of each run, Pallas kernels for 32% -> 35%
where the time goes in v3:
time: 154 us; the launch traced here: 153 us
  Pallas kernels  72.9 us (47%)
  waiting for transfers between devices  38.3 us (25%)
  blocking collectives  20.1 us (13%)
  starting transfers between devices  18.2 us (12%)
    all_to_all x4, waiting for transfers between devices, exchange(): return lax.all_to_all(array, 'frame', 0, 0, tiled=True)  38.3 us
    pallas_call x2, Pallas kernels, window_call(): pl.pallas_call(lambda *refs: window_kernel(n, frames, part, len(pieces),...  35.4 us
    pallas_call x2, Pallas kernels, spatial_call(): pl.pallas_call(lambda *refs: spatial_kernel(n, *refs), grid=(count,), in_...  30.7 us
    all_to_all x1, blocking collectives, exchange(): return lax.all_to_all(array, 'frame', 0, 0, tiled=True)  20.1 us
    all_to_all x4, starting transfers between devices, exchange(): return lax.all_to_all(array, 'frame', 0, 0, tiled=True)  18.2 us
    pallas_call x2, Pallas kernels, place_call(): pl.pallas_call(place_kernel, grid=(frames,), in_specs=[pl.BlockSpec((n, 1...  6.73 us
  transfers between devices with their start and end apart: 4, of which 3 were waited for; matrix products, arithmetic and copies ran while one was open for 0% of the time, Pallas kernels for 35%

profile of v3, /device:TPU:0, one launch (start us, length us, event | category | flops | bytes accessed | tf_op | source)
XLA Modules:
  0.0 153.2 jit_solution(7416744664707743595)
XLA Ops:
  0.0 0.0 copy-start
  0.8 0.3 copy-done
  1.1 0.4 fusion.2
  1.4 1.3 fusion.8
  2.7 15.4 %spatial.2 = (bf16[8,2,4,8,512]{4,3,2,1,0:T(8,128)(2,1)}, bf16[8,4,4,8,512]{4,3,2,1,0:T(8,128)(2,1)}) custom-call(bf16[4,512,512]{2,1,0:T(8,128)(2,1)} %refs_0_.3, f32[1,512]{1,0:T(1,128)} %bitcast.21, f32[1,512]{1,0:T(1,128)} %bitcast.19, bf16[512,1536]{1,0:T(8,128)(2,1)} %refs_3_.3, bf16[512,512]{1,0:T(8,128)(2,1)} %refs_4_.4), custom_call_target="tpu_custom_call" | custom-call | flops 4294967296 | bytes 4194304 | tf_op jit(solution)/shard_map/spatial/pallas_call | solution.py:217
  18.1 7.3 %all-to-all-start.2 = ((bf16[8,2,4,8,512]{4,3,2,1,0:T(8,128)(2,1)}), bf16[8,2,4,8,512]{4,3,2,1,0:T(8,128)(2,1)S(1)}, u32[]{:S(2)}, u32[]{:S(2)}) async-start(bf16[8,2,4,8,512]{4,3,2,1,0:T(8,128)(2,1)} %get-tuple-element.11), calls=%async_computation.2 | async-start | bytes 1048576 | tf_op jit(solution)/shard_map/all_to_all | solution.py:398
  25.4 15.3 %spatial.3 = (bf16[8,2,4,8,512]{4,3,2,1,0:T(8,128)(2,1)}, bf16[8,4,4,8,512]{4,3,2,1,0:T(8,128)(2,1)}) custom-call(bf16[4,512,512]{2,1,0:T(8,128)(2,1)} %refs_0_.3, f32[1,512]{1,0:T(1,128)} %bitcast.22, f32[1,512]{1,0:T(1,128)} %bitcast.20, bf16[512,1536]{1,0:T(8,128)(2,1)} %refs_3_.3, bf16[512,512]{1,0:T(8,128)(2,1)} %refs_4_.4, ...), custom_call_target="tpu_custom_call", output_to_operand_aliasing={{1}: (5, {})} | custom-call | flops 4294967296 | bytes 4194304 | tf_op jit(solution)/shard_map/spatial/pallas_call | solution.py:217
  40.7 0.0 all-to-all-done.2.refs_0_
  40.7 20.1 %all_to_all.25.refs_1_ = bf16[8,2,4,8,512]{4,3,2,1,0:T(8,128)(2,1)} all-to-all(bf16[8,2,4,8,512]{4,3,2,1,0:T(8,128)(2,1)} %get-tuple-element.12), channel_id=1, replica_groups=mesh['clip'=4,'frame'=8] {'frame'}, dimensions={0} | all-to-all | bytes 1048576 | tf_op jit(solution)/shard_map/all_to_all | solution.py:398
  60.8 3.7 %all-to-all-start = ((bf16[8,4,4,8,512]{4,3,2,1,0:T(8,128)(2,1)}), bf16[8,4,4,8,512]{4,3,2,1,0:T(8,128)(2,1)S(1)}, u32[]{:S(2)}, u32[]{:S(2)}) async-start(bf16[8,4,4,8,512]{4,3,2,1,0:T(8,128)(2,1)} %get-tuple-element.10), calls=%async_computation | async-start | bytes 2097152 | tf_op jit(solution)/shard_map/all_to_all | solution.py:398
  64.5 0.0 copy-done.4
  64.5 17.7 %window.3 = bf16[8,4,32,512]{3,2,1,0:T(8,128)(2,1)} custom-call(bf16[8,2,4,8,512]{4,3,2,1,0:T(8,128)(2,1)} %copy-done.4, bf16[8,2,4,8,512]{4,3,2,1,0:T(8,128)(2,1)} %all_to_all.25.refs_1_, f32[1,512]{1,0:T(1,128)} %bitcast.15, f32[1,512]{1,0:T(1,128)} %bitcast.13, f32[1,1024]{1,0:T(1,128)} %bitcast.17, bf16[512,1536]{1,0:T(8,128)(2,1)} %refs_5_.3, ...), custom_call_target="tpu_custom_call" | custom-call | flops 4429185024 | bytes 22020096 | tf_op jit(solution)/shard_map/window/pallas_call | solution.py:326
  82.3 7.7 %all-to-all-done.refs_0_ = bf16[8,4,4,8,512]{4,3,2,1,0:T(8,128)(2,1)S(1)} async-done(((bf16[8,4,4,8,512]{4,3,2,1,0:T(8,128)(2,1)}), bf16[8,4,4,8,512]{4,3,2,1,0:T(8,128)(2,1)S(1)}, u32[]{:S(2)}, u32[]{:S(2)}) %all-to-all-start) | async-done | bytes 1048608 | tf_op jit(solution)/shard_map/all_to_all | solution.py:398
  90.0 0.0 copy-start.1
  90.0 3.6 %all-to-all-start.4 = ((bf16[8,4,32,512]{3,2,1,0:T(8,128)(2,1)}), bf16[8,4,32,512]{3,2,1,0:T(8,128)(2,1)S(1)}, u32[]{:S(2)}, u32[]{:S(2)}) async-start(bf16[8,4,32,512]{3,2,1,0:T(8,128)(2,1)} %window.3), calls=%async_computation.4 | async-start | bytes 2097152 | tf_op jit(solution)/shard_map/all_to_all | solution.py:398
  93.5 0.0 copy-done.1
  93.6 17.7 %window.2 = bf16[8,4,32,512]{3,2,1,0:T(8,128)(2,1)} custom-call(bf16[8,4,4,8,512]{4,3,2,1,0:T(8,128)(2,1)} %copy-done.1, f32[1,512]{1,0:T(1,128)} %bitcast.16, f32[1,512]{1,0:T(1,128)} %bitcast.14, f32[1,1024]{1,0:T(1,128)} %bitcast.18, bf16[512,1536]{1,0:T(8,128)(2,1)} %refs_5_.3, bf16[512,512]{1,0:T(8,128)(2,1)} %refs_6_.3, bf16[4096,1024]{1,0:T(8,128)(2,1)} %refs_7_.3, ...), custom_call_target="tpu_custom_call" | custom-call | flops 4429185024 | bytes 22020096 | tf_op jit(solution)/shard_map/window/pallas_call | solution.py:326
  111.3 8.0 %all-to-all-done.4.piece_ref = bf16[8,4,32,512]{3,2,1,0:T(8,128)(2,1)S(1)} async-done(((bf16[8,4,32,512]{3,2,1,0:T(8,128)(2,1)}), bf16[8,4,32,512]{3,2,1,0:T(8,128)(2,1)S(1)}, u32[]{:S(2)}, u32[]{:S(2)}) %all-to-all-start.4) | async-done | bytes 1048608 | tf_op jit(solution)/shard_map/all_to_all | solution.py:398
  119.3 3.6 %all-to-all-start.1 = ((bf16[8,4,32,512]{3,2,1,0:T(8,128)(2,1)}), bf16[8,4,32,512]{3,2,1,0:T(8,128)(2,1)S(1)}, u32[]{:S(2)}, u32[]{:S(2)}) async-start(bf16[8,4,32,512]{3,2,1,0:T(8,128)(2,1)} %window.2), calls=%async_computation.1 | async-start | bytes 2097152 | tf_op jit(solution)/shard_map/all_to_all | solution.py:398
  122.9 0.0 copy-done.2
  123.0 3.4 %place.2.refs_0_ = bf16[4,8,2,32,512]{4,3,2,1,0:T(8,128)(2,1)} custom-call(bf16[8,4,32,512]{3,2,1,0:T(8,128)(2,1)} %copy-done.2), custom_call_target="tpu_custom_call" | custom-call | bytes 2097152 | tf_op jit(solution)/shard_map/place/pallas_call | solution.py:358
  126.3 22.6 %all-to-all-done.1.piece_ref = bf16[8,4,32,512]{3,2,1,0:T(8,128)(2,1)S(1)} async-done(((bf16[8,4,32,512]{3,2,1,0:T(8,128)(2,1)}), bf16[8,4,32,512]{3,2,1,0:T(8,128)(2,1)S(1)}, u32[]{:S(2)}, u32[]{:S(2)}) %all-to-all-start.1) | async-done | bytes 1048608 | tf_op jit(solution)/shard_map/all_to_all | solution.py:398
  148.9 1.0 copy-done.3
  149.9 3.4 %place.3 = bf16[4,8,2,32,512]{4,3,2,1,0:T(8,128)(2,1)} custom-call(bf16[8,4,32,512]{3,2,1,0:T(8,128)(2,1)} %copy-done.3, bf16[4,8,2,32,512]{4,3,2,1,0:T(8,128)(2,1)} %place.2.refs_0_), custom_call_target="tpu_custom_call", output_to_operand_aliasing={{}: (1, {})} | custom-call | bytes 2097152 | tf_op jit(solution)/shard_map/place/pallas_call | solution.py:358
  (4 shorter events, 0.1 us)
Async XLA Ops:
  0.0 1.1 copy-start
  18.1 22.6 %all-to-all-start.2 = ((bf16[8,2,4,8,512]{4,3,2,1,0:T(8,128)(2,1)}), bf16[8,2,4,8,512]{4,3,2,1,0:T(8,128)(2,1)S(1)}, u32[]{:S(2)}, u32[]{:S(2)}) async-start(bf16[8,2,4,8,512]{4,3,2,1,0:T(8,128)(2,1)} %get-tuple-element.11), calls=%async_computation.2 | async-start | bytes 1048576 | tf_op jit(solution)/shard_map/all_to_all | solution.py:398
  40.7 23.8 %copy-start.4 = (bf16[8,2,4,8,512]{4,3,2,1,0:T(8,128)(2,1)}, bf16[8,2,4,8,512]{4,3,2,1,0:T(8,128)(2,1)S(1)}, u32[]{:S(2)}) copy-start(bf16[8,2,4,8,512]{4,3,2,1,0:T(8,128)(2,1)S(1)} %all-to-all-done.2.refs_0_) | copy-start | bytes 1572868
  60.8 29.2 %all-to-all-start = ((bf16[8,4,4,8,512]{4,3,2,1,0:T(8,128)(2,1)}), bf16[8,4,4,8,512]{4,3,2,1,0:T(8,128)(2,1)S(1)}, u32[]{:S(2)}, u32[]{:S(2)}) async-start(bf16[8,4,4,8,512]{4,3,2,1,0:T(8,128)(2,1)} %get-tuple-element.10), calls=%async_computation | async-start | bytes 2097152 | tf_op jit(solution)/shard_map/all_to_all | solution.py:398
  90.0 3.6 %copy-start.1 = (bf16[8,4,4,8,512]{4,3,2,1,0:T(8,128)(2,1)}, bf16[8,4,4,8,512]{4,3,2,1,0:T(8,128)(2,1)S(1)}, u32[]{:S(2)}) copy-start(bf16[8,4,4,8,512]{4,3,2,1,0:T(8,128)(2,1)S(1)} %all-to-all-done.refs_0_) | copy-start | bytes 3145732
  90.0 29.3 %all-to-all-start.4 = ((bf16[8,4,32,512]{3,2,1,0:T(8,128)(2,1)}), bf16[8,4,32,512]{3,2,1,0:T(8,128)(2,1)S(1)}, u32[]{:S(2)}, u32[]{:S(2)}) async-start(bf16[8,4,32,512]{3,2,1,0:T(8,128)(2,1)} %window.3), calls=%async_computation.4 | async-start | bytes 2097152 | tf_op jit(solution)/shard_map/all_to_all | solution.py:398
  119.3 3.6 %copy-start.2 = (bf16[8,4,32,512]{3,2,1,0:T(8,128)(2,1)}, bf16[8,4,32,512]{3,2,1,0:T(8,128)(2,1)S(1)}, u32[]{:S(2)}) copy-start(bf16[8,4,32,512]{3,2,1,0:T(8,128)(2,1)S(1)} %all-to-all-done.4.piece_ref) | copy-start | bytes 3145732
  119.3 29.6 %all-to-all-start.1 = ((bf16[8,4,32,512]{3,2,1,0:T(8,128)(2,1)}), bf16[8,4,32,512]{3,2,1,0:T(8,128)(2,1)S(1)}, u32[]{:S(2)}, u32[]{:S(2)}) async-start(bf16[8,4,32,512]{3,2,1,0:T(8,128)(2,1)} %window.2), calls=%async_computation.1 | async-start | bytes 2097152 | tf_op jit(solution)/shard_map/all_to_all | solution.py:398
  148.9 1.0 copy-start.3
